TPU v7x, 128 devices: a whole 4x4x4 slice. The times are simulated.
128 devices in a mesh: group: 4 (over y_hi, core), pair: 32 (over x, z, y_lo).
Axes of the slice: x: 4, y: 4 (y_hi: 2, y_lo: 2; y = y_hi * 2 + y_lo), z: 4, core: 2. Of those that a mesh axis runs over, the one named last changes fastest.
Arguments:
- genotypes: int32 [4096, 65536], P(None, ('group', 'pair')), may hold values from 0 to 2, as said below
- dest_group: int32 [256], replicated, may hold values from 0 to 3, as said below
Outputs:
- rotated: bfloat16 [4096, 65536], P(None, ('group', 'pair'))
Inputs may be any that keep to these rules, and one draw needn't show every extreme that they name: For every pair index p and side k there is an offset s with dest_group[(g * 32 + p) * 2 + k] = (g + s) mod 4 for all g, and the two sides have different offsets; so every position (t, p, k) receives exactly one block. `genotypes`: allele counts of two alleles.
All inputs are finite; a program needn't handle non-finite values.
Results may differ from a plain program's by a relative error of at most 0.0077.
Values may be sent and summed in bfloat16 or wider, within the bound.
A program may use at most 128 MiB of HBM per device.

v0:
```python
import jax
import jax.numpy as jnp
from jax import lax
from jax.sharding import PartitionSpec as P

ROUNDS = 3


epsilon = 1e-05


def passed_along(array, axis, by):
    size = lax.axis_size(axis)
    return lax.ppermute(array, axis, [(i, (i + by) % size) for i in range(size)])


def standardize(counts):
    values = counts.astype(jnp.float32)
    col_mean = jnp.mean(values, axis=0)
    centred = values - col_mean
    col_var = jnp.mean(centred * centred, axis=0)
    return (centred / jnp.sqrt(col_var + epsilon)).astype(jnp.bfloat16)


def rotation_for(top_block, low_block):
    blk_width = top_block.shape[1]
    top_wide = top_block.astype(jnp.float32)
    low_wide = low_block.astype(jnp.float32)
    norm_top = jnp.sum(top_wide * top_wide, axis=0)
    norm_low = jnp.sum(low_wide * low_wide, axis=0)
    cross_gram = lax.dot_general(
        top_block, low_block, (((0,), (0,)), ((), ())), preferred_element_type=jnp.float32
    )
    coupling = 2.0 * cross_gram / (norm_top[:, None] + norm_low[None, :] + epsilon)
    zero_block = jnp.zeros((blk_width, blk_width), jnp.float32)
    skew_part = jnp.concatenate(
        [
            jnp.concatenate([zero_block, coupling], axis=1),
            jnp.concatenate([-coupling.T, zero_block], axis=1),
        ],
        axis=0,
    )
    identity = jnp.eye(2 * blk_width, dtype=jnp.float32)
    gram_matrix = identity + jnp.dot(skew_part.T, skew_part, precision=lax.Precision.HIGHEST)
    factor = jnp.linalg.cholesky(gram_matrix)
    lifted = identity + skew_part
    rotation = jax.scipy.linalg.solve_triangular(factor, lifted.T, lower=True).T
    return rotation.astype(jnp.bfloat16)


def body(genotypes, dest_group):
    num_groups = lax.axis_size("group")
    num_pairs = lax.axis_size("pair")
    own_group = lax.axis_index("group")
    own_pair = lax.axis_index("pair")
    blk_width = genotypes.shape[1] // 2
    scaled = standardize(genotypes)
    first_block = scaled[:, :blk_width]
    second_block = scaled[:, blk_width:]
    dest_table = dest_group.reshape(num_groups, num_pairs, 2)
    column = lax.dynamic_index_in_dim(dest_table, own_pair, 1, keepdims=False)
    own_dest = lax.dynamic_index_in_dim(column, own_group, 0, keepdims=False)
    groups_iota = jnp.arange(num_groups, dtype=jnp.int32)
    source_zero = jnp.sum(jnp.where(column[:, 0] == own_group, groups_iota, 0))
    source_one = jnp.sum(jnp.where(column[:, 1] == own_group, groups_iota, 0))
    pick_zero = (groups_iota == own_dest[0])[:, None, None]
    pick_one = (groups_iota == own_dest[1])[:, None, None]
    send_slots = jnp.where(
        pick_zero,
        first_block[None],
        jnp.where(pick_one, second_block[None], jnp.zeros_like(first_block)[None]),
    )
    arrived = lax.all_to_all(send_slots, "group", split_axis=0, concat_axis=0, tiled=True)
    top_block = lax.dynamic_index_in_dim(arrived, source_zero, 0, keepdims=False)
    low_block = lax.dynamic_index_in_dim(arrived, source_one, 0, keepdims=False)
    for cycle_round in range(ROUNDS):
        rotation = rotation_for(top_block, low_block)
        joined = jnp.concatenate([top_block, low_block], axis=1)
        result = jnp.dot(joined, rotation, preferred_element_type=jnp.float32).astype(jnp.bfloat16)
        top_block = result[:, :blk_width]
        low_block = passed_along(result[:, blk_width:], "pair", 1)
    return jnp.concatenate([top_block, low_block], axis=1)


def solution(mesh):
    in_specs = (P(None, ("group", "pair")), P())
    out_specs = P(None, ("group", "pair"))
    return jax.shard_map(body, mesh=mesh, in_specs=in_specs, out_specs=out_specs, check_vma=False)
```

profile of v0, /device:TPU:1, one launch (start us, length us, event | category | flops | bytes accessed | tf_op | source)
XLA Modules:
  0.0 737.3 jit_solution(18264324090191979567)
XLA Ops:
  27.8 88.5 %all-to-all-done = bf16[4,4096,256]{2,1,0:T(8,128)(2,1)} async-done(((bf16[4,4096,256]{2,1,0:T(8,128)(2,1)}), bf16[4,4096,256]{2,1,0:T(8,128)(2,1)}, u32[]{:S(2)}, u32[]{:S(2)}) %all-to-all-start) | async-done | bytes 8388640 | tf_op jit(solution)/shard_map/all_to_all | solution.py:73
  127.0 11.7 %cholesky.374 = f32[128,128]{1,0:T(8,128)S(1)} custom-call(f32[128,128]{1,0:T(8,128)S(1)} %cholesky.586), custom_call_target="Cholesky" | custom-call | tf_op jit(solution)/shard_map/jit(cholesky)/cholesky | solution.py:45
  138.9 9.8 %custom-call.31 = f32[1,128,128]{1,2,0:T(8,128)S(1)} custom-call(f32[1,128,128]{2,1,0:T(8,128)S(1)} %get-tuple-element.105), custom_call_target="InvertDiagBlocksLowerTriangular" | custom-call | tf_op jit(solution)/shard_map/jit(cholesky)/cholesky | solution.py:45
  151.2 12.1 %cholesky.393 = f32[128,128]{1,0:T(8,128)S(1)} custom-call(f32[128,128]{1,0:T(8,128)S(1)} %cholesky.590), custom_call_target="Cholesky" | custom-call | tf_op jit(solution)/shard_map/jit(cholesky)/cholesky | solution.py:45
  176.1 11.7 %cholesky.414 = f32[128,128]{1,0:T(8,128)S(1)} custom-call(f32[128,128]{1,0:T(8,128)S(1)} %cholesky.595), custom_call_target="Cholesky" | custom-call | tf_op jit(solution)/shard_map/jit(cholesky)/cholesky | solution.py:45
  188.6 9.9 %custom-call.33 = f32[1,128,128]{1,2,0:T(8,128)S(1)} custom-call(f32[1,128,128]{2,1,0:T(8,128)S(1)} %get-tuple-element.99), custom_call_target="InvertDiagBlocksLowerTriangular" | custom-call | tf_op jit(solution)/shard_map/jit(cholesky)/cholesky | solution.py:45
  200.0 11.7 %cholesky.431 = f32[128,128]{1,0:T(8,128)S(1)} custom-call(f32[128,128]{1,0:T(8,128)S(1)} %convolution_subtract_fusion.17), custom_call_target="Cholesky" | custom-call | tf_op jit(solution)/shard_map/jit(cholesky)/cholesky | solution.py:45
  223.0 39.3 %custom-call.34 = f32[4,128,128]{1,2,0:T(8,128)S(1)} custom-call(f32[4,128,128]{2,1,0:T(8,128)S(1)} %get-tuple-element.27), custom_call_target="InvertDiagBlocksLowerTriangular" | custom-call | tf_op jit(solution)/shard_map/jit(_solve_triangular)/triangular_solve | solution.py:47
  279.9 48.7 %collective-permute-done = bf16[4096,256]{1,0:T(8,128)(2,1)S(1)} collective-permute-done((bf16[4096,256]{1,0:T(8,128)(2,1)}, bf16[4096,256]{1,0:T(8,128)(2,1)S(1)}, u32[]{:S(2)}, u32[]{:S(2)}) %collective-permute-start) | collective-permute-done | bytes 2097184 | tf_op jit(solution)/shard_map/ppermute | solution.py:14
  337.9 11.7 %cholesky.446 = f32[128,128]{1,0:T(8,128)S(1)} custom-call(f32[128,128]{1,0:T(8,128)S(1)} %cholesky.599), custom_call_target="Cholesky" | custom-call | tf_op jit(solution)/shard_map/jit(cholesky)/cholesky | solution.py:45
  349.8 9.8 %custom-call.35 = f32[1,128,128]{1,2,0:T(8,128)S(1)} custom-call(f32[1,128,128]{2,1,0:T(8,128)S(1)} %get-tuple-element.95), custom_call_target="InvertDiagBlocksLowerTriangular" | custom-call | tf_op jit(solution)/shard_map/jit(cholesky)/cholesky | solution.py:45
  362.1 11.9 %cholesky.465 = f32[128,128]{1,0:T(8,128)S(1)} custom-call(f32[128,128]{1,0:T(8,128)S(1)} %cholesky.603), custom_call_target="Cholesky" | custom-call | tf_op jit(solution)/shard_map/jit(cholesky)/cholesky | solution.py:45
  386.8 11.7 %cholesky.486 = f32[128,128]{1,0:T(8,128)S(1)} custom-call(f32[128,128]{1,0:T(8,128)S(1)} %cholesky.608), custom_call_target="Cholesky" | custom-call | tf_op jit(solution)/shard_map/jit(cholesky)/cholesky | solution.py:45
  410.8 11.7 %cholesky.503 = f32[128,128]{1,0:T(8,128)S(1)} custom-call(f32[128,128]{1,0:T(8,128)S(1)} %convolution_subtract_fusion.16), custom_call_target="Cholesky" | custom-call | tf_op jit(solution)/shard_map/jit(cholesky)/cholesky | solution.py:45
  433.9 39.3 %custom-call.38 = f32[4,128,128]{1,2,0:T(8,128)S(1)} custom-call(f32[4,128,128]{2,1,0:T(8,128)S(1)} %get-tuple-element.28), custom_call_target="InvertDiagBlocksLowerTriangular" | custom-call | tf_op jit(solution)/shard_map/jit(_solve_triangular)/triangular_solve | solution.py:47
  483.0 49.3 %collective-permute-done.1 = bf16[4096,256]{1,0:T(8,128)(2,1)S(1)} collective-permute-done((bf16[4096,256]{1,0:T(8,128)(2,1)S(1)}, bf16[4096,256]{1,0:T(8,128)(2,1)S(1)}, u32[]{:S(2)}, u32[]{:S(2)}) %collective-permute-start.1) | collective-permute-done | bytes 2097184 | tf_op jit(solution)/shard_map/ppermute | solution.py:14
  537.7 11.7 %cholesky.518 = f32[128,128]{1,0:T(8,128)S(1)} custom-call(f32[128,128]{1,0:T(8,128)S(1)} %cholesky.612), custom_call_target="Cholesky" | custom-call | tf_op jit(solution)/shard_map/jit(cholesky)/cholesky | solution.py:45
  549.5 9.8 %custom-call.39 = f32[1,128,128]{1,2,0:T(8,128)S(1)} custom-call(f32[1,128,128]{2,1,0:T(8,128)S(1)} %get-tuple-element.85), custom_call_target="InvertDiagBlocksLowerTriangular" | custom-call | tf_op jit(solution)/shard_map/jit(cholesky)/cholesky | solution.py:45
  561.9 11.9 %cholesky.537 = f32[128,128]{1,0:T(8,128)S(1)} custom-call(f32[128,128]{1,0:T(8,128)S(1)} %cholesky.616), custom_call_target="Cholesky" | custom-call | tf_op jit(solution)/shard_map/jit(cholesky)/cholesky | solution.py:45
  575.1 9.8 %custom-call.40 = f32[1,128,128]{1,2,0:T(8,128)S(1)} custom-call(f32[1,128,128]{2,1,0:T(8,128)S(1)} %get-tuple-element.82), custom_call_target="InvertDiagBlocksLowerTriangular" | custom-call | tf_op jit(solution)/shard_map/jit(cholesky)/cholesky | solution.py:45
  586.5 11.7 %cholesky.558 = f32[128,128]{1,0:T(8,128)S(1)} custom-call(f32[128,128]{1,0:T(8,128)S(1)} %cholesky.621), custom_call_target="Cholesky" | custom-call | tf_op jit(solution)/shard_map/jit(cholesky)/cholesky | solution.py:45
  610.2 11.9 %cholesky.575 = f32[128,128]{1,0:T(8,128)S(1)} custom-call(f32[128,128]{1,0:T(8,128)S(1)} %convolution_subtract_fusion.15), custom_call_target="Cholesky" | custom-call | tf_op jit(solution)/shard_map/jit(cholesky)/cholesky | solution.py:45
  633.3 39.3 %custom-call.42 = f32[4,128,128]{1,2,0:T(8,128)S(1)} custom-call(f32[4,128,128]{2,1,0:T(8,128)S(1)} %get-tuple-element.29), custom_call_target="InvertDiagBlocksLowerTriangular" | custom-call | tf_op jit(solution)/shard_map/jit(_solve_triangular)/triangular_solve | solution.py:47
  679.0 49.0 %collective-permute-done.2 = bf16[4096,256]{0,1:T(8,128)(2,1)S(1)} collective-permute-done((bf16[4096,256]{0,1:T(8,128)(2,1)S(1)}, bf16[4096,256]{0,1:T(8,128)(2,1)S(1)}, u32[]{:S(2)}, u32[]{:S(2)}) %collective-permute-start.2) | collective-permute-done | bytes 2097184 | tf_op jit(solution)/shard_map/ppermute | solution.py:14
  (214 shorter events, 203.2 us)
Async XLA Ops:
  1.5 5.8 copy-start
  15.6 100.7 %all-to-all-start = ((bf16[4,4096,256]{2,1,0:T(8,128)(2,1)}), bf16[4,4096,256]{2,1,0:T(8,128)(2,1)}, u32[]{:S(2)}, u32[]{:S(2)}) async-start(bf16[4,4096,256]{2,1,0:T(8,128)(2,1)} %select_select_fusion), calls=%async_computation | async-start | bytes 16777216 | tf_op jit(solution)/shard_map/all_to_all | solution.py:73
  119.6 1.4 copy-start.5
  119.7 2.0 copy-start.7
  122.9 0.7 copy-start.15
  126.0 1.0 copy-start.2
  262.3 2.7 copy-start.16
  262.3 7.7 %copy-start.6 = (bf16[4096,256]{1,0:T(8,128)(2,1)S(1)}, bf16[4096,256]{1,0:T(8,128)(2,1)}, u32[]{:S(2)}) copy-start(bf16[4096,256]{1,0:T(8,128)(2,1)} %copy-done.5) | copy-start | bytes 6291460
  262.3 7.7 %copy-start.8 = (bf16[4096,256]{1,0:T(8,128)(2,1)S(1)}, bf16[4096,256]{1,0:T(8,128)(2,1)}, u32[]{:S(2)}) copy-start(bf16[4096,256]{1,0:T(8,128)(2,1)} %copy-done.7) | copy-start | bytes 6291460
  272.7 3.3 copy-start.1
  275.9 52.7 %collective-permute-start = (bf16[4096,256]{1,0:T(8,128)(2,1)}, bf16[4096,256]{1,0:T(8,128)(2,1)S(1)}, u32[]{:S(2)}, u32[]{:S(2)}) collective-permute-start(bf16[4096,256]{1,0:T(8,128)(2,1)} %get-tuple-element.73), channel_id=1, source_target_pairs={{0,1},{1,2},{2,3},{3,4},{4,5},{5,6},{6,7},{7,8},{8,9},{9,10},{10,1... | collective-permute-start | bytes 6291464 | tf_op jit(solution)/shard_map/ppermute | solution.py:14
  328.6 5.8 copy-start.11
  336.9 1.0 copy-start.3
  473.2 4.8 copy-start.12
  473.2 4.8 copy-start.14
  482.3 50.0 %collective-permute-start.1 = (bf16[4096,256]{1,0:T(8,128)(2,1)S(1)}, bf16[4096,256]{1,0:T(8,128)(2,1)S(1)}, u32[]{:S(2)}, u32[]{:S(2)}) collective-permute-start(bf16[4096,256]{1,0:T(8,128)(2,1)S(1)} %get-tuple-element.71), channel_id=1, source_target_pairs={{0,1},{1,2},{2,3},{3,4},{4,5},{5,6},{6,7},{7,8},{8,9},{9,10},{10,1... | collective-permute-start | bytes 6291464 | tf_op jit(solution)/shard_map/ppermute | solution.py:14
  532.3 1.9 copy-start.9
  536.7 1.0 copy-start.4
  672.6 3.2 copy-start.10
  672.6 3.2 copy-start.13
  678.9 49.1 %collective-permute-start.2 = (bf16[4096,256]{0,1:T(8,128)(2,1)S(1)}, bf16[4096,256]{0,1:T(8,128)(2,1)S(1)}, u32[]{:S(2)}, u32[]{:S(2)}) collective-permute-start(bf16[4096,256]{0,1:T(8,128)(2,1)S(1)} %get-tuple-element.69), channel_id=1, source_target_pairs={{0,1},{1,2},{2,3},{3,4},{4,5},{5,6},{6,7},{7,8},{8,9},{9,10},{10,1... | collective-permute-start | bytes 6291464 | tf_op jit(solution)/shard_map/ppermute | solution.py:14
where the time goes:
time: 744 us; the launch traced here: 737 us
  other arithmetic  383 us (51%)
  waiting for transfers between devices  236 us (32%)
  matrix products  49.1 us (7%)
  local copies, waits for them, and re-layouts  47.1 us (6%)
  between operations  13.2 us (2%)
  starting transfers between devices  9.2 us (1%)
    another operation x45, other arithmetic, rotation_for(): factor = jnp.linalg.cholesky(gram_matrix)  238 us
    ppermute x3, waiting for transfers between devices, passed_along(): lax.ppermute(array, axis, [(i, (i + by) % size) for i in range(size)])  147 us
    another operation x7, other arithmetic, rotation_for(): rotation = jax.scipy.linalg.solve_triangular(factor, lifted.T, lower=True).T  118 us
    all_to_all x1, waiting for transfers between devices, body(): lax.all_to_all(send_slots, 'group', split_axis=0, concat_axis=0, tiled=True)  88.5 us
    another operation x40, local copies, waits for them, and re-layouts, rotation_for(): rotation = jax.scipy.linalg.solve_triangular(factor, lifted.T, lower=True).T  23.4 us
    another operation x18, matrix products, rotation_for(): factor = jnp.linalg.cholesky(gram_matrix)  16.4 us
  transfers between devices with their start and end apart: 4, of which 4 were waited for; matrix products, arithmetic and copies ran while one was open for 1% of the time, Pallas kernels for 0%

commit v1 on v0

--- a/solution.py
+++ b/solution.py
@@ -1,10 +1,13 @@
 import jax
 import jax.numpy as jnp
 from jax import lax
+from jax.experimental import pallas as pl
+from jax.experimental.pallas import tpu as pltpu
 from jax.sharding import PartitionSpec as P
 
 ROUNDS = 3
-
+HALF = 64
+CHUNK = 512
 
 epsilon = 1e-05
 
@@ -22,30 +25,112 @@
     return (centred / jnp.sqrt(col_var + epsilon)).astype(jnp.bfloat16)
 
 
-def rotation_for(top_block, low_block):
-    blk_width = top_block.shape[1]
-    top_wide = top_block.astype(jnp.float32)
-    low_wide = low_block.astype(jnp.float32)
-    norm_top = jnp.sum(top_wide * top_wide, axis=0)
-    norm_low = jnp.sum(low_wide * low_wide, axis=0)
-    cross_gram = lax.dot_general(
-        top_block, low_block, (((0,), (0,)), ((), ())), preferred_element_type=jnp.float32
+def product(left, right, left_dim, right_dim):
+    dims = (((left_dim,), (right_dim,)), ((), ()))
+    return lax.dot_general(
+        left, right, dims, precision=lax.Precision.HIGHEST, preferred_element_type=jnp.float32
     )
-    coupling = 2.0 * cross_gram / (norm_top[:, None] + norm_low[None, :] + epsilon)
-    zero_block = jnp.zeros((blk_width, blk_width), jnp.float32)
-    skew_part = jnp.concatenate(
-        [
-            jnp.concatenate([zero_block, coupling], axis=1),
-            jnp.concatenate([-coupling.T, zero_block], axis=1),
+
+
+def inverse_factor_pair(rows):
+    lane = lax.broadcasted_iota(jnp.int32, (8, 128), 1)
+    sub = lax.broadcasted_iota(jnp.int32, (8, 128), 0)
+    start = jnp.where(lane < HALF, 0, HALF)
+    col = lane - start
+    rows = list(rows)
+    for j in range(HALF):
+        tile, s = divmod(j, 8)
+        index = start + j
+        here = col == j
+        pivot_row = jnp.broadcast_to(rows[tile][s : s + 1, :], (8, 128))
+        inverse = 1.0 / jnp.take_along_axis(pivot_row, index, axis=1)
+        scaled = jnp.where(here, 1.0, pivot_row) * inverse
+        for r in range(tile if s < 7 else tile + 1, 8):
+            ratio = jnp.take_along_axis(rows[r], index, axis=1)
+            update = jnp.where(here, 0.0, rows[r]) - ratio * scaled
+            rows[r] = jnp.where(sub > s, update, rows[r]) if r == tile else update
+    done = []
+    for r in range(8):
+        row = sub + 8 * r
+        scale = lax.rsqrt(jnp.take_along_axis(rows[r], start + row, axis=1))
+        done.append(jnp.where(col < row, rows[r] * scale, jnp.where(col == row, scale, 0.0)))
+    return jnp.concatenate(done, axis=0)
+
+
+def invert_factors(gram):
+    width = gram.shape[1]
+    eye_row = lax.broadcasted_iota(jnp.int32, (HALF, HALF), 0)
+    eye = (eye_row == lax.broadcasted_iota(jnp.int32, (HALF, HALF), 1)).astype(jnp.float32)
+    lanes = lax.broadcasted_iota(jnp.int32, (HALF, width), 1)
+    for low in range(0, width, HALF):
+        high = low + HALF
+        block = jnp.concatenate([gram[m, low:high, low:high] for m in range(2)], axis=1)
+        both = inverse_factor_pair([block[8 * r : 8 * r + 8] for r in range(8)])
+        for m in range(2):
+            gram[m, low:high, low:high] = eye
+            panel = product(both[:, HALF * m : HALF * m + HALF], gram[m, low:high, :], 1, 0)
+            if high < width:
+                gram[m, high:, low:high] = jnp.zeros((width - high, HALF), jnp.float32)
+                gram[m, high:, :] = gram[m, high:, :] - product(panel[:, high:], panel, 0, 0)
+                panel = jnp.where(lanes < high, panel, 0.0)
+            gram[m, low:high, :] = panel
+
+
+def rotate_kernel(top_ref, low_ref, new_top_ref, new_low_ref, gram, cross, norm, turn):
+    rows, width = top_ref.shape
+    cross[...] = jnp.zeros_like(cross)
+    norm[...] = jnp.zeros_like(norm)
+
+    @pl.loop(0, rows // CHUNK)
+    def _(i):
+        part = pl.ds(pl.multiple_of(i * CHUNK, CHUNK), CHUNK)
+        top, low = top_ref[part, :], low_ref[part, :]
+        cross[...] += lax.dot_general(
+            top, low, (((0,), (0,)), ((), ())), preferred_element_type=jnp.float32
+        )
+        for m, block in enumerate((top, low)):
+            wide = block.astype(jnp.float32)
+            norm[m] += jnp.sum((wide * wide).reshape(CHUNK // 8, 8, width), axis=0)
+
+    norm_top = jnp.broadcast_to(jnp.sum(norm[0], axis=0, keepdims=True), (width, width)).T
+    norm_low = jnp.sum(norm[1], axis=0, keepdims=True)
+    coupling = 2.0 * cross[...] / (norm_top + norm_low + epsilon)
+    cross[...] = coupling
+    row = lax.broadcasted_iota(jnp.int32, (width, width), 0)
+    eye = (row == lax.broadcasted_iota(jnp.int32, (width, width), 1)).astype(jnp.float32)
+    gram[0] = eye + product(coupling, coupling, 1, 1)
+    gram[1] = eye + product(coupling, coupling, 0, 0)
+    invert_factors(gram)
+    turn[0:width, 0:width] = gram[0].T.astype(jnp.bfloat16)
+    turn[0:width, width:] = product(cross[...], gram[1], 1, 1).astype(jnp.bfloat16)
+    turn[width:, 0:width] = (-product(cross[...], gram[0], 0, 1)).astype(jnp.bfloat16)
+    turn[width:, width:] = gram[1].T.astype(jnp.bfloat16)
+
+    @pl.loop(0, rows // CHUNK)
+    def _(i):
+        part = pl.ds(pl.multiple_of(i * CHUNK, CHUNK), CHUNK)
+        joined = jnp.concatenate([top_ref[part, :], low_ref[part, :]], axis=1)
+        result = jnp.dot(joined, turn[...], preferred_element_type=jnp.float32).astype(jnp.bfloat16)
+        new_top_ref[part, :] = result[:, :width]
+        new_low_ref[part, :] = result[:, width:]
+
+
+def rotate(top, low):
+    width = top.shape[1]
+    vmem = pl.BlockSpec(memory_space=pltpu.VMEM)
+    return pl.pallas_call(
+        rotate_kernel,
+        out_shape=[jax.ShapeDtypeStruct(top.shape, top.dtype)] * 2,
+        in_specs=[vmem, vmem],
+        out_specs=[vmem, vmem],
+        scratch_shapes=[
+            pltpu.VMEM((2, width, width), jnp.float32),
+            pltpu.VMEM((width, width), jnp.float32),
+            pltpu.VMEM((2, 8, width), jnp.float32),
+            pltpu.VMEM((2 * width, 2 * width), jnp.bfloat16),
         ],
-        axis=0,
-    )
-    identity = jnp.eye(2 * blk_width, dtype=jnp.float32)
-    gram_matrix = identity + jnp.dot(skew_part.T, skew_part, precision=lax.Precision.HIGHEST)
-    factor = jnp.linalg.cholesky(gram_matrix)
-    lifted = identity + skew_part
-    rotation = jax.scipy.linalg.solve_triangular(factor, lifted.T, lower=True).T
-    return rotation.astype(jnp.bfloat16)
+        compiler_params=pltpu.CompilerParams(vmem_limit_bytes=32 * 2**20),
+    )(top, low)
 
 
 def body(genotypes, dest_group):
@@ -74,11 +159,8 @@
     top_block = lax.dynamic_index_in_dim(arrived, source_zero, 0, keepdims=False)
     low_block = lax.dynamic_index_in_dim(arrived, source_one, 0, keepdims=False)
     for cycle_round in range(ROUNDS):
-        rotation = rotation_for(top_block, low_block)
-        joined = jnp.concatenate([top_block, low_block], axis=1)
-        result = jnp.dot(joined, rotation, preferred_element_type=jnp.float32).astype(jnp.bfloat16)
-        top_block = result[:, :blk_width]
-        low_block = passed_along(result[:, blk_width:], "pair", 1)
+        top_block, low_block = rotate(top_block, low_block)
+        low_block = passed_along(low_block, "pair", 1)
     return jnp.concatenate([top_block, low_block], axis=1)
 
 

time: 744 us -> 371 us (0.50)
  other arithmetic: 383 us -> 18.3 us
  Pallas kernels: 0 us -> 93.7 us
  matrix products: 49.1 us -> 0 us
  local copies, waits for them, and re-layouts: 47.1 us -> 5.24 us
  between operations: 13.2 us -> 3.91 us
    another operation x52 -> x0, other arithmetic: 357 us -> none  [the longest x45 238 us: rotation_for(): factor = jnp.linalg.cholesky(gram_matrix)]
    pallas_call x0 -> x3, Pallas kernels: none -> 93.7 us  [rotate(): pl.pallas_call(rotate_kernel, out_shape=[jax.ShapeDtypeStruct(top.shape,...]
    another operation x39 -> x0, matrix products: 30.7 us -> none  [the longest x18 16.4 us: rotation_for(): factor = jnp.linalg.cholesky(gram_matrix)]
    another operation x52 -> x0, local copies, waits for them, and re-layouts: 23.8 us -> none  [the longest x40 23.4 us: rotation_for(): rotation = jax.scipy.linalg.solve_triangular(factor, lifted.T, lower=True).T]
    dot_general x9 -> x0, matrix products: 18.4 us -> none  [the longest x3 7.87 us: body(): jnp.dot(joined, rotation, preferred_element_type=jnp.float32)]
  transfers between devices with their start and end apart: 4 -> 4, of which waited for: 4 -> 4; matrix products, arithmetic and copies ran while one was open for 1% -> 0% of each run, Pallas kernels for 0% -> 0%
where the time goes in v1:
time: 371 us; the launch traced here: 369 us
  waiting for transfers between devices  239 us (64%)
  Pallas kernels  93.7 us (25%)
  other arithmetic  18.3 us (5%)
  starting transfers between devices  9.08 us (2%)
  local copies, waits for them, and re-layouts  5.24 us (1%)
  between operations  3.91 us (1%)
    ppermute x3, waiting for transfers between devices, passed_along(): lax.ppermute(array, axis, [(i, (i + by) % size) for i in range(size)])  150 us
    pallas_call x3, Pallas kernels, rotate(): pl.pallas_call(rotate_kernel, out_shape=[jax.ShapeDtypeStruct(top.shape,...  93.7 us
    all_to_all x1, waiting for transfers between devices, body(): lax.all_to_all(send_slots, 'group', split_axis=0, concat_axis=0, tiled=True)  89.2 us
  transfers between devices with their start and end apart: 4, of which 4 were waited for; matrix products, arithmetic and copies ran while one was open for 0% of the time, Pallas kernels for 0%

profile of v1, /device:TPU:1, one launch (start us, length us, event | category | flops | bytes accessed | tf_op | source)
XLA Modules:
  0.0 369.0 jit_solution(2821794971134004355)
XLA Ops:
  0.0 4.1 %convert_reduce_fusion = f32[512]{0:T(512)S(1)} fusion(s32[4096,512]{1,0:T(8,128)} %param.2), kind=kLoop, calls=%fused_computation.4 | loop fusion | flops 4193792 | bytes 8390656 | tf_op jit(solution)/shard_map/reduce_sum | solution.py:22
  4.2 1.6 copy-done
  5.8 1.2 multiply_reduce_fusion
  6.9 0.1 reshape.31
  7.1 0.6 fusion.3
  7.7 4.6 %divide_convert_fusion = bf16[4096,512]{1,0:T(8,128)(2,1)S(1)} fusion(s32[4096,512]{1,0:T(8,128)} %param.2, f32[512]{0:T(512)S(1)} %add_sqrt_fusion, f32[512]{0:T(512)S(1)} %broadcast_multiply_fusion), kind=kLoop, calls=%fused_computation.1 | loop fusion | flops 8388608 | bytes 12587008 | tf_op jit(solution)/shard_map/convert_element_type | solution.py:25
  12.3 0.3 fusion.2
  12.6 1.3 iota_compare_fusion
  13.8 4.2 %select_select_fusion = bf16[4,4096,256]{2,1,0:T(8,128)(2,1)} fusion(pred[4]{0:T(512)(128)(4,1)S(1)} %get-tuple-element.25, pred[4]{0:T(512)(128)(4,1)S(1)} %get-tuple-element.26, bf16[4096,256]{1,0:T(8,128)(2,1)S(1)} %get-tuple-element.22, bf16[4096,256]{1,0:T(8,128)(2,1)S(1)} %get-tuple-element.21), kind=kLoop, calls=%fused_computation | loop fusion | flops 8388608 | bytes 12582920 | tf_op jit(solution)/shard_map/jit(_where)/select_n | solution.py:153
  18.0 7.0 %all-to-all-start = ((bf16[4,4096,256]{2,1,0:T(8,128)(2,1)}), bf16[4,4096,256]{2,1,0:T(8,128)(2,1)}, u32[]{:S(2)}, u32[]{:S(2)}) async-start(bf16[4,4096,256]{2,1,0:T(8,128)(2,1)} %select_select_fusion), calls=%async_computation | async-start | bytes 16777216 | tf_op jit(solution)/shard_map/all_to_all | solution.py:158
  25.0 0.1 copy.3
  25.1 0.6 fusion.1
  29.5 89.2 %all-to-all-done = bf16[4,4096,256]{2,1,0:T(8,128)(2,1)} async-done(((bf16[4,4096,256]{2,1,0:T(8,128)(2,1)}), bf16[4,4096,256]{2,1,0:T(8,128)(2,1)}, u32[]{:S(2)}, u32[]{:S(2)}) %all-to-all-start) | async-done | bytes 8388640 | tf_op jit(solution)/shard_map/all_to_all | solution.py:158
  118.7 2.5 dynamic-slice_bitcast_fusion
  121.2 31.2 %shard_map.28 = (bf16[4096,256]{1,0:T(8,128)(2,1)S(1)}, bf16[4096,256]{1,0:T(8,128)(2,1)S(1)}) custom-call(bf16[4096,256]{1,0:T(8,128)(2,1)S(1)} %get-tuple-element.20.top_ref, bf16[4096,256]{1,0:T(8,128)(2,1)S(1)} %get-tuple-element.19.low_ref), custom_call_target="tpu_custom_call" | custom-call | tf_op jit(solution)/shard_map/pallas_call | solution.py:121
  152.5 1.7 collective-permute-start
  154.2 50.7 %collective-permute-done.low_ref = bf16[4096,256]{1,0:T(8,128)(2,1)S(1)} collective-permute-done((bf16[4096,256]{1,0:T(8,128)(2,1)S(1)}, bf16[4096,256]{1,0:T(8,128)(2,1)S(1)}, u32[]{:S(2)}, u32[]{:S(2)}) %collective-permute-start) | collective-permute-done | bytes 2097184 | tf_op jit(solution)/shard_map/ppermute | solution.py:17
  204.9 31.3 %shard_map.29 = (bf16[4096,256]{1,0:T(8,128)(2,1)S(1)}, bf16[4096,256]{1,0:T(8,128)(2,1)S(1)}) custom-call(bf16[4096,256]{1,0:T(8,128)(2,1)S(1)} %get-tuple-element.11.top_ref, bf16[4096,256]{1,0:T(8,128)(2,1)S(1)} %collective-permute-done.low_ref), custom_call_target="tpu_custom_call" | custom-call | tf_op jit(solution)/shard_map/pallas_call | solution.py:121
  236.1 0.3 collective-permute-start.1
  236.5 49.8 %collective-permute-done.1.low_ref = bf16[4096,256]{1,0:T(8,128)(2,1)S(1)} collective-permute-done((bf16[4096,256]{1,0:T(8,128)(2,1)S(1)}, bf16[4096,256]{1,0:T(8,128)(2,1)S(1)}, u32[]{:S(2)}, u32[]{:S(2)}) %collective-permute-start.1) | collective-permute-done | bytes 2097184 | tf_op jit(solution)/shard_map/ppermute | solution.py:17
  286.3 31.2 %shard_map.30 = (bf16[4096,256]{1,0:T(8,128)(2,1)S(1)}, bf16[4096,256]{1,0:T(8,128)(2,1)S(1)}) custom-call(bf16[4096,256]{1,0:T(8,128)(2,1)S(1)} %get-tuple-element.13.top_ref, bf16[4096,256]{1,0:T(8,128)(2,1)S(1)} %collective-permute-done.1.low_ref), custom_call_target="tpu_custom_call" | custom-call | tf_op jit(solution)/shard_map/pallas_call | solution.py:121
  317.6 0.1 collective-permute-start.2
  317.6 49.0 %collective-permute-done.2 = bf16[4096,256]{1,0:T(8,128)(2,1)S(1)} collective-permute-done((bf16[4096,256]{1,0:T(8,128)(2,1)S(1)}, bf16[4096,256]{1,0:T(8,128)(2,1)S(1)}, u32[]{:S(2)}, u32[]{:S(2)}) %collective-permute-start.2) | collective-permute-done | bytes 2097184 | tf_op jit(solution)/shard_map/ppermute | solution.py:17
  366.6 2.3 pad_maximum_fusion
  (7 shorter events, 0.0 us)
Async XLA Ops:
  0.0 5.8 %copy-start = (s32[4096,512]{1,0:T(8,128)S(1)}, s32[4096,512]{1,0:T(8,128)}, u32[]{:S(2)}) copy-start(s32[4096,512]{1,0:T(8,128)} %param.2) | copy-start | bytes 25165828
  5.8 1.2 copy-start.1
  18.0 100.7 %all-to-all-start = ((bf16[4,4096,256]{2,1,0:T(8,128)(2,1)}), bf16[4,4096,256]{2,1,0:T(8,128)(2,1)}, u32[]{:S(2)}, u32[]{:S(2)}) async-start(bf16[4,4096,256]{2,1,0:T(8,128)(2,1)} %select_select_fusion), calls=%async_computation | async-start | bytes 16777216 | tf_op jit(solution)/shard_map/all_to_all | solution.py:158
  152.5 52.4 %collective-permute-start = (bf16[4096,256]{1,0:T(8,128)(2,1)S(1)}, bf16[4096,256]{1,0:T(8,128)(2,1)S(1)}, u32[]{:S(2)}, u32[]{:S(2)}) collective-permute-start(bf16[4096,256]{1,0:T(8,128)(2,1)S(1)} %get-tuple-element.12), channel_id=1, source_target_pairs={{0,1},{1,2},{2,3},{3,4},{4,5},{5,6},{6,7},{7,8},{8,9},{9,10},{10,1... | collective-permute-start | bytes 6291464 | tf_op jit(solution)/shard_map/ppermute | solution.py:17
  236.1 50.2 %collective-permute-start.1 = (bf16[4096,256]{1,0:T(8,128)(2,1)S(1)}, bf16[4096,256]{1,0:T(8,128)(2,1)S(1)}, u32[]{:S(2)}, u32[]{:S(2)}) collective-permute-start(bf16[4096,256]{1,0:T(8,128)(2,1)S(1)} %get-tuple-element.14), channel_id=1, source_target_pairs={{0,1},{1,2},{2,3},{3,4},{4,5},{5,6},{6,7},{7,8},{8,9},{9,10},{10,1... | collective-permute-start | bytes 6291464 | tf_op jit(solution)/shard_map/ppermute | solution.py:17
  317.6 49.1 %collective-permute-start.2 = (bf16[4096,256]{1,0:T(8,128)(2,1)S(1)}, bf16[4096,256]{1,0:T(8,128)(2,1)S(1)}, u32[]{:S(2)}, u32[]{:S(2)}) collective-permute-start(bf16[4096,256]{1,0:T(8,128)(2,1)S(1)} %get-tuple-element.16), channel_id=1, source_target_pairs={{0,1},{1,2},{2,3},{3,4},{4,5},{5,6},{6,7},{7,8},{8,9},{9,10},{10,1... | collective-permute-start | bytes 6291464 | tf_op jit(solution)/shard_map/ppermute | solution.py:17

commit v2 on v1

--- a/solution.py
+++ b/solution.py
@@ -12,11 +12,6 @@
 epsilon = 1e-05
 
 
-def passed_along(array, axis, by):
-    size = lax.axis_size(axis)
-    return lax.ppermute(array, axis, [(i, (i + by) % size) for i in range(size)])
-
-
 def standardize(counts):
     values = counts.astype(jnp.float32)
     col_mean = jnp.mean(values, axis=0)
@@ -32,27 +27,39 @@
     )
 
 
+def spread(tile, row):
+    return jnp.broadcast_to(tile[row : row + 1, :], tile.shape)
+
+
 def inverse_factor_pair(rows):
     lane = lax.broadcasted_iota(jnp.int32, (8, 128), 1)
     sub = lax.broadcasted_iota(jnp.int32, (8, 128), 0)
     start = jnp.where(lane < HALF, 0, HALF)
     col = lane - start
     rows = list(rows)
-    for j in range(HALF):
-        tile, s = divmod(j, 8)
-        index = start + j
-        here = col == j
-        pivot_row = jnp.broadcast_to(rows[tile][s : s + 1, :], (8, 128))
-        inverse = 1.0 / jnp.take_along_axis(pivot_row, index, axis=1)
-        scaled = jnp.where(here, 1.0, pivot_row) * inverse
-        for r in range(tile if s < 7 else tile + 1, 8):
-            ratio = jnp.take_along_axis(rows[r], index, axis=1)
-            update = jnp.where(here, 0.0, rows[r]) - ratio * scaled
-            rows[r] = jnp.where(sub > s, update, rows[r]) if r == tile else update
+    pivots = [jnp.ones((8, 128), jnp.float32)] * 8
+    for first in range(0, HALF, 8):
+        tile = first // 8
+        cols = [
+            [jnp.take_along_axis(rows[r], start + (first + m), axis=1) for r in range(tile, 8)]
+            for m in range(8)
+        ]
+        for m in range(8):
+            here = col == first + m
+            pivot = spread(cols[m][0], m)
+            inverse = 1.0 / pivot
+            pivots[tile] = jnp.where(sub == m, pivot, pivots[tile])
+            cols[m][0] = jnp.where(sub > m, cols[m][0], 0.0)
+            for n in range(m + 1, 8):
+                ratio = spread(cols[n][0], m) * inverse
+                cols[n] = [c - f * ratio for c, f in zip(cols[n], cols[m])]
+            scaled = jnp.where(here, 1.0, spread(rows[tile], m)) * inverse
+            for r in range(tile, 8):
+                rows[r] = jnp.where(here, 0.0, rows[r]) - cols[m][r - tile] * scaled
     done = []
     for r in range(8):
         row = sub + 8 * r
-        scale = lax.rsqrt(jnp.take_along_axis(rows[r], start + row, axis=1))
+        scale = lax.rsqrt(pivots[r])
         done.append(jnp.where(col < row, rows[r] * scale, jnp.where(col == row, scale, 0.0)))
     return jnp.concatenate(done, axis=0)
 
@@ -133,35 +140,195 @@
     )(top, low)
 
 
+def ring_place(y, core):
+    y = lax.rem(y + 4, 4)
+    column = lax.axis_index("pair") // 2
+    return {"group": (y // 2) * 2 + core, "pair": column * 2 + lax.rem(y, 2)}
+
+
+def own_ring_position():
+    group, pair = lax.axis_index("group"), lax.axis_index("pair")
+    return (group // 2) * 2 + lax.rem(pair, 2), lax.rem(group, 2)
+
+
+def regroup_kernel(choice, slots, top_ref, low_ref, landed, passed, send, recv, pass_send):
+    y, core = own_ring_position()
+    side = lax.rem(y, 2)
+    chunks = recv.shape[1]
+    rows = slots.shape[1] // chunks
+
+    barrier = pltpu.get_barrier_semaphore()
+    for step in (1, -1):
+        for other in range(2):
+            pl.semaphore_signal(barrier, inc=1, device_id=ring_place(y + step, other))
+    pl.semaphore_signal(barrier, inc=1, device_id=ring_place(y, 1 - core))
+    pl.semaphore_wait(barrier, 5)
+
+    def part(i):
+        return pl.ds(i * rows, rows)
+
+    def away(slot, i):
+        step = 1 if slot == 1 else -1
+        place = core if slot == 1 else 2 + core
+        return pltpu.make_async_remote_copy(
+            src_ref=slots.at[slot, part(i)],
+            dst_ref=landed.at[place, part(i)],
+            send_sem=send.at[slot, i],
+            recv_sem=recv.at[place, i],
+            device_id=ring_place(y + step, side),
+        )
+
+    def across(i):
+        return pltpu.make_async_remote_copy(
+            src_ref=slots.at[0, part(i)],
+            dst_ref=landed.at[core, part(i)],
+            send_sem=send.at[0, i],
+            recv_sem=recv.at[core, i],
+            device_id=ring_place(y, 1 - core),
+        )
+
+    def stay(i):
+        return pltpu.make_async_copy(slots.at[0, part(i)], landed.at[core, part(i)], recv.at[core, i])
+
+    def onward(way, i):
+        return pltpu.make_async_remote_copy(
+            src_ref=passed.at[way, part(i)],
+            dst_ref=landed.at[2 + way, part(i)],
+            send_sem=pass_send.at[way, i],
+            recv_sem=recv.at[2 + way, i],
+            device_id=ring_place(y + (1 if way == 0 else -1), core),
+        )
+
+    def arrival(place, i):
+        here = landed.at[place, part(i)]
+        pltpu.make_async_copy(here, here, recv.at[place, i]).wait()
+
+    for i in range(chunks):
+        for slot in (1, 2):
+            away(slot, i).start()
+
+    @pl.when(core == side)
+    def _():
+        for i in range(chunks):
+            stay(i).start()
+
+    @pl.when(core != side)
+    def _():
+        for i in range(chunks):
+            across(i).start()
+
+    for i in range(chunks):
+        for place in range(4):
+            arrival(place, i)
+            if place % 2 == 1:
+                way = place // 2
+
+                @pl.when(core != side)
+                def _():
+                    first, second = landed[2 * way, part(i)], landed[2 * way + 1, part(i)]
+                    passed[way, part(i)] = jnp.where(choice[way] > 0, second, first)
+                    onward(way, i).start()
+
+        for place, out in ((2, top_ref), (3, low_ref)):
+            which = choice[place]
+            lower = jnp.where(which == 0, landed[0, part(i)], landed[1, part(i)])
+            upper = jnp.where(which == 2, landed[2, part(i)], landed[3, part(i)])
+            out[part(i), :] = jnp.where(which < 2, lower, upper)
+
+    for i in range(chunks):
+        for slot in (1, 2):
+            away(slot, i).wait_send()
+
+        @pl.when(core != side)
+        def _():
+            across(i).wait_send()
+            for way in range(2):
+                onward(way, i).wait_send()
+
+
+def regroup(slots, choice):
+    _, rows, width = slots.shape
+    vmem = pl.BlockSpec(memory_space=pltpu.VMEM)
+    chunks = 4
+    return pl.pallas_call(
+        regroup_kernel,
+        out_shape=[jax.ShapeDtypeStruct((rows, width), slots.dtype)] * 2,
+        in_specs=[pl.BlockSpec(memory_space=pltpu.SMEM), pl.BlockSpec(memory_space=pl.ANY)],
+        out_specs=[vmem, vmem],
+        scratch_shapes=[
+            pltpu.VMEM((4, rows, width), slots.dtype),
+            pltpu.VMEM((2, rows, width), slots.dtype),
+            pltpu.SemaphoreType.DMA((3, chunks)),
+            pltpu.SemaphoreType.DMA((4, chunks)),
+            pltpu.SemaphoreType.DMA((2, chunks)),
+        ],
+        compiler_params=pltpu.CompilerParams(
+            collective_id=0, has_side_effects=True, vmem_limit_bytes=32 * 2**20
+        ),
+    )(choice, slots)
+
+
+def slot_codes(dest_group):
+    table = dest_group.reshape(4, 32, 2)
+    chip = (jnp.arange(4)[:, None] // 2) * 2 + jnp.arange(32)[None, :] % 2
+    distance = (table - chip[:, :, None] + 4) % 4
+    other = distance[:, :, ::-1]
+    slot = jnp.where(distance == 3, 2, distance)
+    slot = jnp.where(distance == 2, jnp.where(other == 1, 2, 1), slot)
+    return table, distance, slot
+
+
+def choices(table, distance, slot):
+    y, core = own_ring_position()
+    column = lax.axis_index("pair") // 2
+    pair = column * 2 + core
+    dist, slots, dest = (
+        lax.dynamic_index_in_dim(array, pair, 1, keepdims=False) for array in (distance, slot, table)
+    )
+    far = jnp.where(dist == 2, slots, 0)
+    after, before = ((y + 3) % 4) // 2 * 2 + 1, ((y + 1) % 4) // 2 * 2 + 1
+    second = jnp.arange(4)
+    pass_up = jnp.sum(jnp.where((second == after)[:, None] & (far == 1), 1, 0))
+    pass_down = jnp.sum(jnp.where((second == before)[:, None] & (far == 2), 1, 0))
+    origin = second % 2
+    place = jnp.where(
+        dist % 2 == 1,
+        origin[:, None] + jnp.where(dist == 1, 0, 2),
+        jnp.where(dist == 0, origin[:, None], 1 + slots),
+    )
+    wanted = jnp.sum(jnp.where(dest == y, place, 0), axis=0)
+    return jnp.stack([pass_up, pass_down, wanted[0], wanted[1]]).astype(jnp.int32)
+
+
+def home(t, p):
+    return t * 32 + p
+
+
+def working_place(t, p):
+    return ((t // 2) * 2 + p % 2) * 32 + (p // 2) * 2 + t % 2
+
+
+def moved(array, source, target, by):
+    pairs = [(source(t, p), target(t, (p + by) % 32)) for t in range(4) for p in range(32)]
+    return lax.ppermute(array, ("group", "pair"), pairs)
+
+
 def body(genotypes, dest_group):
-    num_groups = lax.axis_size("group")
-    num_pairs = lax.axis_size("pair")
-    own_group = lax.axis_index("group")
-    own_pair = lax.axis_index("pair")
-    blk_width = genotypes.shape[1] // 2
+    width = genotypes.shape[1] // 2
     scaled = standardize(genotypes)
-    first_block = scaled[:, :blk_width]
-    second_block = scaled[:, blk_width:]
-    dest_table = dest_group.reshape(num_groups, num_pairs, 2)
-    column = lax.dynamic_index_in_dim(dest_table, own_pair, 1, keepdims=False)
-    own_dest = lax.dynamic_index_in_dim(column, own_group, 0, keepdims=False)
-    groups_iota = jnp.arange(num_groups, dtype=jnp.int32)
-    source_zero = jnp.sum(jnp.where(column[:, 0] == own_group, groups_iota, 0))
-    source_one = jnp.sum(jnp.where(column[:, 1] == own_group, groups_iota, 0))
-    pick_zero = (groups_iota == own_dest[0])[:, None, None]
-    pick_one = (groups_iota == own_dest[1])[:, None, None]
-    send_slots = jnp.where(
-        pick_zero,
-        first_block[None],
-        jnp.where(pick_one, second_block[None], jnp.zeros_like(first_block)[None]),
-    )
-    arrived = lax.all_to_all(send_slots, "group", split_axis=0, concat_axis=0, tiled=True)
-    top_block = lax.dynamic_index_in_dim(arrived, source_zero, 0, keepdims=False)
-    low_block = lax.dynamic_index_in_dim(arrived, source_one, 0, keepdims=False)
+    table, distance, slot = slot_codes(dest_group)
+    own_slot = lax.dynamic_index_in_dim(slot, lax.axis_index("pair"), 1, keepdims=False)
+    own_slot = lax.dynamic_index_in_dim(own_slot, lax.axis_index("group"), 0, keepdims=False)
+    takes_first = (jnp.arange(3) == own_slot[0])[:, None, None]
+    slots = jnp.where(takes_first, scaled[None, :, :width], scaled[None, :, width:])
+    top, low = regroup(slots, choices(table, distance, slot))
     for cycle_round in range(ROUNDS):
-        top_block, low_block = rotate(top_block, low_block)
-        low_block = passed_along(low_block, "pair", 1)
-    return jnp.concatenate([top_block, low_block], axis=1)
+        top, low = rotate(top, low)
+        if cycle_round < ROUNDS - 1:
+            low = moved(low, working_place, working_place, 1)
+    top = moved(top, working_place, home, 0)
+    low = moved(low, working_place, home, 1)
+    return jnp.concatenate([top, low], axis=1)
 
 
 def solution(mesh):

time: 371 us -> 253 us (0.68)
  waiting for transfers between devices: 239 us -> 93.9 us
  Pallas kernels: 93.7 us -> 122 us
  starting transfers between devices: 9.08 us -> 17.5 us
  between operations: 3.91 us -> 0.16 us
    all_to_all x1 -> x0, waiting for transfers between devices: 89.2 us -> none  [body(): lax.all_to_all(send_slots, 'group', split_axis=0, concat_axis=0, tiled=True)]
    pallas_call x0 -> x1, Pallas kernels: none -> 73 us  [regroup(): pl.pallas_call(regroup_kernel, out_shape=[jax.ShapeDtypeStruct((rows, wid...]
    ppermute x3 -> x4, waiting for transfers between devices: 150 us -> 93.9 us  [moved(): return lax.ppermute(array, ('group', 'pair'), pairs)]
    pallas_call x3, Pallas kernels: 93.7 us -> 49.3 us  [rotate(): pl.pallas_call(rotate_kernel, out_shape=[jax.ShapeDtypeStruct(top.shape,...]
    ppermute x3 -> x4, starting transfers between devices: 2.11 us -> 17.5 us  [moved(): return lax.ppermute(array, ('group', 'pair'), pairs)]
    all_to_all x1 -> x0, starting transfers between devices: 6.97 us -> none  [body(): lax.all_to_all(send_slots, 'group', split_axis=0, concat_axis=0, tiled=True)]
where the time goes in v2:
time: 253 us; the launch traced here: 252 us
  Pallas kernels  122 us (48%)
  waiting for transfers between devices  93.9 us (37%)
  starting transfers between devices  17.5 us (7%)
  other arithmetic  15.4 us (6%)
  local copies, waits for them, and re-layouts  3.09 us (1%)
    ppermute x4, waiting for transfers between devices, moved(): return lax.ppermute(array, ('group', 'pair'), pairs)  93.9 us
    pallas_call x1, Pallas kernels, regroup(): pl.pallas_call(regroup_kernel, out_shape=[jax.ShapeDtypeStruct((rows, wid...  73 us
    pallas_call x3, Pallas kernels, rotate(): pl.pallas_call(rotate_kernel, out_shape=[jax.ShapeDtypeStruct(top.shape,...  49.3 us
    ppermute x4, starting transfers between devices, moved(): return lax.ppermute(array, ('group', 'pair'), pairs)  17.5 us
  transfers between devices with their start and end apart: 4, of which 4 were waited for; matrix products, arithmetic and copies ran while one was open for 0% of the time, Pallas kernels for 0%

profile of v2, /device:TPU:1, one launch (start us, length us, event | category | flops | bytes accessed | tf_op | source)
XLA Modules:
  0.0 252.3 jit_solution(6503203784038949628)
XLA Ops:
  0.0 0.8 reshape.121
  0.9 0.1 add_select_fusion
  1.2 4.1 %convert_reduce_fusion = f32[512]{0:T(512)S(1)} fusion(s32[4096,512]{1,0:T(8,128)} %param.2), kind=kLoop, calls=%fused_computation.3 | loop fusion | flops 4193792 | bytes 8390656 | tf_op jit(solution)/shard_map/reduce_sum | solution.py:17
  5.3 1.6 copy-done
  6.9 1.2 multiply_reduce_fusion
  8.1 0.1 copy.12
  8.3 0.1 fusion.1
  8.6 4.6 %divide_convert_fusion = bf16[4096,512]{1,0:T(8,128)(2,1)S(1)} fusion(s32[4096,512]{1,0:T(8,128)} %param.2, f32[512]{0:T(512)S(1)} %add_sqrt_fusion, f32[512]{0:T(512)S(1)} %broadcast_multiply_fusion), kind=kLoop, calls=%fused_computation | loop fusion | flops 8388608 | bytes 12587008 | tf_op jit(solution)/shard_map/convert_element_type | solution.py:20
  13.2 0.3 fusion.8
  13.4 0.8 fusion.2
  14.2 1.4 pad_add_fusion.choice
  15.6 0.7 broadcast_select_fusion.slots
  16.3 73.0 %shard_map.28 = (bf16[4096,256]{1,0:T(8,128)(2,1)S(1)}, bf16[4096,256]{1,0:T(8,128)(2,1)S(1)}) custom-call(s32[4]{0:T(128)S(1)} %pad_add_fusion.choice, bf16[3,4096,256]{2,1,0:T(8,128)(2,1)S(1)} %broadcast_select_fusion.slots), custom_call_target="tpu_custom_call" | custom-call | tf_op jit(solution)/shard_map/pallas_call | solution.py:253
  89.3 16.4 %shard_map.29 = (bf16[4096,256]{1,0:T(8,128)(2,1)S(1)}, bf16[4096,256]{1,0:T(8,128)(2,1)S(1)}) custom-call(bf16[4096,256]{1,0:T(8,128)(2,1)S(1)} %get-tuple-element.13.top_ref, bf16[4096,256]{1,0:T(8,128)(2,1)S(1)} %get-tuple-element.14.low_ref), custom_call_target="tpu_custom_call" | custom-call | tf_op jit(solution)/shard_map/pallas_call | solution.py:128
  105.7 3.6 %collective-permute-start = (bf16[4096,256]{1,0:T(8,128)(2,1)S(1)}, bf16[4096,256]{1,0:T(8,128)(2,1)S(1)}, u32[]{:S(2)}, u32[]{:S(2)}) collective-permute-start(bf16[4096,256]{1,0:T(8,128)(2,1)S(1)} %get-tuple-element.16), channel_id=1, source_target_pairs={{0,32},{32,2},{2,34},{34,4},{4,36},{36,6},{6,38},{38,8},{8,40},{40... | collective-permute-start | bytes 6291464 | tf_op jit(solution)/shard_map/ppermute | solution.py:313
  109.3 23.0 %collective-permute-done.low_ref = bf16[4096,256]{1,0:T(8,128)(2,1)S(1)} collective-permute-done((bf16[4096,256]{1,0:T(8,128)(2,1)S(1)}, bf16[4096,256]{1,0:T(8,128)(2,1)S(1)}, u32[]{:S(2)}, u32[]{:S(2)}) %collective-permute-start) | collective-permute-done | bytes 2097184 | tf_op jit(solution)/shard_map/ppermute | solution.py:313
  132.3 16.4 %shard_map.30 = (bf16[4096,256]{1,0:T(8,128)(2,1)S(1)}, bf16[4096,256]{1,0:T(8,128)(2,1)S(1)}) custom-call(bf16[4096,256]{1,0:T(8,128)(2,1)S(1)} %get-tuple-element.15.top_ref, bf16[4096,256]{1,0:T(8,128)(2,1)S(1)} %collective-permute-done.low_ref), custom_call_target="tpu_custom_call" | custom-call | tf_op jit(solution)/shard_map/pallas_call | solution.py:128
  148.7 2.8 %collective-permute-start.1 = (bf16[4096,256]{1,0:T(8,128)(2,1)S(1)}, bf16[4096,256]{1,0:T(8,128)(2,1)S(1)}, u32[]{:S(2)}, u32[]{:S(2)}) collective-permute-start(bf16[4096,256]{1,0:T(8,128)(2,1)S(1)} %get-tuple-element.18), channel_id=1, source_target_pairs={{0,32},{32,2},{2,34},{34,4},{4,36},{36,6},{6,38},{38,8},{8,40},{40... | collective-permute-start | bytes 6291464 | tf_op jit(solution)/shard_map/ppermute | solution.py:313
  151.6 23.0 %collective-permute-done.1.low_ref = bf16[4096,256]{1,0:T(8,128)(2,1)S(1)} collective-permute-done((bf16[4096,256]{1,0:T(8,128)(2,1)S(1)}, bf16[4096,256]{1,0:T(8,128)(2,1)S(1)}, u32[]{:S(2)}, u32[]{:S(2)}) %collective-permute-start.1) | collective-permute-done | bytes 2097184 | tf_op jit(solution)/shard_map/ppermute | solution.py:313
  174.5 16.4 %shard_map.31 = (bf16[4096,256]{1,0:T(8,128)(2,1)S(1)}, bf16[4096,256]{1,0:T(8,128)(2,1)S(1)}) custom-call(bf16[4096,256]{1,0:T(8,128)(2,1)S(1)} %get-tuple-element.17.top_ref, bf16[4096,256]{1,0:T(8,128)(2,1)S(1)} %collective-permute-done.1.low_ref), custom_call_target="tpu_custom_call" | custom-call | tf_op jit(solution)/shard_map/pallas_call | solution.py:128
  191.0 11.0 %collective-permute-start.2 = (bf16[4096,256]{1,0:T(8,128)(2,1)S(1)}, bf16[4096,256]{1,0:T(8,128)(2,1)S(1)}, u32[]{:S(2)}, u32[]{:S(2)}) collective-permute-start(bf16[4096,256]{1,0:T(8,128)(2,1)S(1)} %get-tuple-element.19), channel_id=1, source_target_pairs={{0,0},{32,1},{2,2},{34,3},{4,4},{36,5},{6,6},{38,7},{8,8},{40,9},{... | collective-permute-start | bytes 6291464 | tf_op jit(solution)/shard_map/ppermute | solution.py:313
  202.1 44.6 %collective-permute-done.2 = bf16[4096,256]{1,0:T(8,128)(2,1)S(1)} collective-permute-done((bf16[4096,256]{1,0:T(8,128)(2,1)S(1)}, bf16[4096,256]{1,0:T(8,128)(2,1)S(1)}, u32[]{:S(2)}, u32[]{:S(2)}) %collective-permute-start.2) | collective-permute-done | bytes 2097184 | tf_op jit(solution)/shard_map/ppermute | solution.py:313
  246.7 3.3 %collective-permute-done.3 = bf16[4096,256]{1,0:T(8,128)(2,1)S(1)} collective-permute-done((bf16[4096,256]{1,0:T(8,128)(2,1)S(1)}, bf16[4096,256]{1,0:T(8,128)(2,1)S(1)}, u32[]{:S(2)}, u32[]{:S(2)}) %collective-permute-start.3) | collective-permute-done | bytes 2097184 | tf_op jit(solution)/shard_map/ppermute | solution.py:313
  250.0 2.3 pad_maximum_fusion
  (16 shorter events, 0.5 us)
Async XLA Ops:
  1.1 5.8 %copy-start = (s32[4096,512]{1,0:T(8,128)S(1)}, s32[4096,512]{1,0:T(8,128)}, u32[]{:S(2)}) copy-start(s32[4096,512]{1,0:T(8,128)} %param.2) | copy-start | bytes 25165828
  105.7 26.6 %collective-permute-start = (bf16[4096,256]{1,0:T(8,128)(2,1)S(1)}, bf16[4096,256]{1,0:T(8,128)(2,1)S(1)}, u32[]{:S(2)}, u32[]{:S(2)}) collective-permute-start(bf16[4096,256]{1,0:T(8,128)(2,1)S(1)} %get-tuple-element.16), channel_id=1, source_target_pairs={{0,32},{32,2},{2,34},{34,4},{4,36},{36,6},{6,38},{38,8},{8,40},{40... | collective-permute-start | bytes 6291464 | tf_op jit(solution)/shard_map/ppermute | solution.py:313
  148.7 25.8 %collective-permute-start.1 = (bf16[4096,256]{1,0:T(8,128)(2,1)S(1)}, bf16[4096,256]{1,0:T(8,128)(2,1)S(1)}, u32[]{:S(2)}, u32[]{:S(2)}) collective-permute-start(bf16[4096,256]{1,0:T(8,128)(2,1)S(1)} %get-tuple-element.18), channel_id=1, source_target_pairs={{0,32},{32,2},{2,34},{34,4},{4,36},{36,6},{6,38},{38,8},{8,40},{40... | collective-permute-start | bytes 6291464 | tf_op jit(solution)/shard_map/ppermute | solution.py:313
  191.0 55.7 %collective-permute-start.2 = (bf16[4096,256]{1,0:T(8,128)(2,1)S(1)}, bf16[4096,256]{1,0:T(8,128)(2,1)S(1)}, u32[]{:S(2)}, u32[]{:S(2)}) collective-permute-start(bf16[4096,256]{1,0:T(8,128)(2,1)S(1)} %get-tuple-element.19), channel_id=1, source_target_pairs={{0,0},{32,1},{2,2},{34,3},{4,4},{36,5},{6,6},{38,7},{8,8},{40,9},{... | collective-permute-start | bytes 6291464 | tf_op jit(solution)/shard_map/ppermute | solution.py:313
  202.0 48.0 %collective-permute-start.3 = (bf16[4096,256]{1,0:T(8,128)(2,1)S(1)}, bf16[4096,256]{1,0:T(8,128)(2,1)S(1)}, u32[]{:S(2)}, u32[]{:S(2)}) collective-permute-start(bf16[4096,256]{1,0:T(8,128)(2,1)S(1)} %get-tuple-element.20), channel_id=1, source_target_pairs={{0,1},{32,2},{2,3},{34,4},{4,5},{36,6},{6,7},{38,8},{8,9},{40,10},... | collective-permute-start | bytes 6291464 | tf_op jit(solution)/shard_map/ppermute | solution.py:313

commit v3 on v2

--- a/solution.py
+++ b/solution.py
@@ -83,22 +83,8 @@
             gram[m, low:high, :] = panel
 
 
-def rotate_kernel(top_ref, low_ref, new_top_ref, new_low_ref, gram, cross, norm, turn):
-    rows, width = top_ref.shape
-    cross[...] = jnp.zeros_like(cross)
-    norm[...] = jnp.zeros_like(norm)
-
-    @pl.loop(0, rows // CHUNK)
-    def _(i):
-        part = pl.ds(pl.multiple_of(i * CHUNK, CHUNK), CHUNK)
-        top, low = top_ref[part, :], low_ref[part, :]
-        cross[...] += lax.dot_general(
-            top, low, (((0,), (0,)), ((), ())), preferred_element_type=jnp.float32
-        )
-        for m, block in enumerate((top, low)):
-            wide = block.astype(jnp.float32)
-            norm[m] += jnp.sum((wide * wide).reshape(CHUNK // 8, 8, width), axis=0)
-
+def rotation_into(turn, gram, cross, norm):
+    width = cross.shape[0]
     norm_top = jnp.broadcast_to(jnp.sum(norm[0], axis=0, keepdims=True), (width, width)).T
     norm_low = jnp.sum(norm[1], axis=0, keepdims=True)
     coupling = 2.0 * cross[...] / (norm_top + norm_low + epsilon)
@@ -113,30 +99,171 @@
     turn[width:, 0:width] = (-product(cross[...], gram[0], 0, 1)).astype(jnp.bfloat16)
     turn[width:, width:] = gram[1].T.astype(jnp.bfloat16)
 
-    @pl.loop(0, rows // CHUNK)
+
+def rounds_kernel(
+    top_in, low_in, top_out, low_out,
+    top, lows, staged, gram, cross, norm, turn, local, send, recv, top_send, top_recv, low_send, low_recv,
+):
+    rows, width = top.shape
+    chunks = rows // CHUNK
+    y, core = own_ring_position()
+    y_low = lax.rem(y, 2)
+    y_base = y - y_low
+    column = lax.axis_index("pair") // 2
+    ahead = lax.rem(column + core, 16)
+    behind = lax.rem(column + core + 15, 16)
+
+    def device(column, y, core):
+        return {"group": (y // 2) * 2 + core, "pair": column * 2 + lax.rem(y, 2)}
+
+    next_device = device(ahead, y, 1 - core)
+    last_device = device(behind, y, 1 - core)
+    top_device = device(column, y_base + core, y_low)
+    low_device = device(ahead, y_base + 1 - core, y_low)
+    low_source = device(lax.rem(column + y_low + 15, 16), y_base + core, 1 - y_low)
+
+    barrier = pltpu.get_barrier_semaphore()
+    for other in (next_device, last_device, low_device, low_source):
+        pl.semaphore_signal(barrier, inc=1, device_id=other)
+
+    @pl.when(core != y_low)
+    def _():
+        pl.semaphore_signal(barrier, inc=1, device_id=top_device)
+        pl.semaphore_wait(barrier, 5)
+
+    @pl.when(core == y_low)
+    def _():
+        pl.semaphore_wait(barrier, 4)
+
+    def part(i):
+        return pl.ds(pl.multiple_of(i * CHUNK, CHUNK), CHUNK)
+
+    first_top = pltpu.make_async_copy(top_in, top, local.at[0])
+    first_low = pltpu.make_async_copy(low_in, lows.at[0], local.at[1])
+    first_top.start()
+    first_low.start()
+    first_top.wait()
+    first_low.wait()
+
+    def shift(r, i):
+        return pltpu.make_async_remote_copy(
+            src_ref=staged.at[r, part(i)],
+            dst_ref=lows.at[r + 1, part(i)],
+            send_sem=send.at[r, i],
+            recv_sem=recv.at[r, i],
+            device_id=next_device,
+        )
+
+    def top_home(i):
+        return pltpu.make_async_remote_copy(
+            src_ref=top.at[part(i)],
+            dst_ref=top_out.at[part(i)],
+            send_sem=top_send.at[i],
+            recv_sem=top_recv.at[i],
+            device_id=top_device,
+        )
+
+    def top_stays(i):
+        return pltpu.make_async_copy(top.at[part(i)], top_out.at[part(i)], top_recv.at[i])
+
+    def low_home(i):
+        return pltpu.make_async_remote_copy(
+            src_ref=staged.at[ROUNDS - 1, part(i)],
+            dst_ref=low_out.at[part(i)],
+            send_sem=low_send.at[i],
+            recv_sem=low_recv.at[i],
+            device_id=low_device,
+        )
+
+    @pl.loop(0, ROUNDS)
+    def _(r):
+        cross[...] = jnp.zeros_like(cross)
+        norm[...] = jnp.zeros_like(norm)
+
+        @pl.loop(0, chunks)
+        def _(i):
+            @pl.when(r > 0)
+            def _():
+                shift(r - 1, i).wait_recv()
+
+            blocks = top[part(i), :], lows[r, part(i), :]
+            cross[...] += lax.dot_general(
+                *blocks, (((0,), (0,)), ((), ())), preferred_element_type=jnp.float32
+            )
+            for m, block in enumerate(blocks):
+                wide = block.astype(jnp.float32)
+                norm[m] += jnp.sum((wide * wide).reshape(CHUNK // 8, 8, width), axis=0)
+
+        rotation_into(turn, gram, cross, norm)
+
+        @pl.loop(0, chunks)
+        def _(i):
+            joined = jnp.concatenate([top[part(i), :], lows[r, part(i), :]], axis=1)
+            result = jnp.dot(joined, turn[...], preferred_element_type=jnp.float32)
+            result = result.astype(jnp.bfloat16)
+            staged[r, part(i), :] = result[:, width:]
+            top[part(i), :] = result[:, :width]
+
+            @pl.when(r < ROUNDS - 1)
+            def _():
+                shift(r, i).start()
+
+            @pl.when(r == ROUNDS - 1)
+            def _():
+                low_home(i).start()
+
+                @pl.when(core != y_low)
+                def _():
+                    top_home(i).start()
+
+                @pl.when(core == y_low)
+                def _():
+                    top_stays(i).start()
+
+    @pl.loop(0, chunks)
     def _(i):
-        part = pl.ds(pl.multiple_of(i * CHUNK, CHUNK), CHUNK)
-        joined = jnp.concatenate([top_ref[part, :], low_ref[part, :]], axis=1)
-        result = jnp.dot(joined, turn[...], preferred_element_type=jnp.float32).astype(jnp.bfloat16)
-        new_top_ref[part, :] = result[:, :width]
-        new_low_ref[part, :] = result[:, width:]
-
-
-def rotate(top, low):
-    width = top.shape[1]
-    vmem = pl.BlockSpec(memory_space=pltpu.VMEM)
+        for r in range(ROUNDS - 1):
+            shift(r, i).wait_send()
+        low_home(i).wait()
+
+        @pl.when(core != y_low)
+        def _():
+            top_home(i).wait()
+
+        @pl.when(core == y_low)
+        def _():
+            top_stays(i).wait()
+
+
+def play_rounds(top, low):
+    rows, width = top.shape
+    chunks = rows // CHUNK
+    anywhere = pl.BlockSpec(memory_space=pl.ANY)
+    dma = pltpu.SemaphoreType.DMA
     return pl.pallas_call(
-        rotate_kernel,
+        rounds_kernel,
         out_shape=[jax.ShapeDtypeStruct(top.shape, top.dtype)] * 2,
-        in_specs=[vmem, vmem],
-        out_specs=[vmem, vmem],
+        in_specs=[anywhere, anywhere],
+        out_specs=[anywhere, anywhere],
         scratch_shapes=[
+            pltpu.VMEM((rows, width), top.dtype),
+            pltpu.VMEM((ROUNDS, rows, width), top.dtype),
+            pltpu.VMEM((ROUNDS, rows, width), top.dtype),
             pltpu.VMEM((2, width, width), jnp.float32),
             pltpu.VMEM((width, width), jnp.float32),
             pltpu.VMEM((2, 8, width), jnp.float32),
             pltpu.VMEM((2 * width, 2 * width), jnp.bfloat16),
+            dma((2,)),
+            dma((ROUNDS - 1, chunks)),
+            dma((ROUNDS - 1, chunks)),
+            dma((chunks,)),
+            dma((chunks,)),
+            dma((chunks,)),
+            dma((chunks,)),
         ],
-        compiler_params=pltpu.CompilerParams(vmem_limit_bytes=32 * 2**20),
+        compiler_params=pltpu.CompilerParams(
+            collective_id=1, has_side_effects=True, vmem_limit_bytes=40 * 2**20
+        ),
     )(top, low)
 
 
@@ -300,19 +427,6 @@
     return jnp.stack([pass_up, pass_down, wanted[0], wanted[1]]).astype(jnp.int32)
 
 
-def home(t, p):
-    return t * 32 + p
-
-
-def working_place(t, p):
-    return ((t // 2) * 2 + p % 2) * 32 + (p // 2) * 2 + t % 2
-
-
-def moved(array, source, target, by):
-    pairs = [(source(t, p), target(t, (p + by) % 32)) for t in range(4) for p in range(32)]
-    return lax.ppermute(array, ("group", "pair"), pairs)
-
-
 def body(genotypes, dest_group):
     width = genotypes.shape[1] // 2
     scaled = standardize(genotypes)
@@ -322,12 +436,7 @@
     takes_first = (jnp.arange(3) == own_slot[0])[:, None, None]
     slots = jnp.where(takes_first, scaled[None, :, :width], scaled[None, :, width:])
     top, low = regroup(slots, choices(table, distance, slot))
-    for cycle_round in range(ROUNDS):
-        top, low = rotate(top, low)
-        if cycle_round < ROUNDS - 1:
-            low = moved(low, working_place, working_place, 1)
-    top = moved(top, working_place, home, 0)
-    low = moved(low, working_place, home, 1)
+    top, low = play_rounds(top, low)
     return jnp.concatenate([top, low], axis=1)
 
 

time: 253 us -> 211 us (0.83)
  waiting for transfers between devices: 93.9 us -> 0 us
  Pallas kernels: 122 us -> 193 us
  starting transfers between devices: 17.5 us -> 0 us
    ppermute x4 -> x0, waiting for transfers between devices: 93.9 us -> none  [moved(): return lax.ppermute(array, ('group', 'pair'), pairs)]
    pallas_call x3 -> x1, Pallas kernels: 49.3 us -> 120 us  [play_rounds(): pl.pallas_call(rounds_kernel, out_shape=[jax.ShapeDtypeStruct(top.shape,...]
    ppermute x4 -> x0, starting transfers between devices: 17.5 us -> none  [moved(): return lax.ppermute(array, ('group', 'pair'), pairs)]
  transfers between devices with their start and end apart: 4 -> 0, of which waited for: 4 -> 0; matrix products, arithmetic and copies ran while one was open for 0% -> 0% of each run, Pallas kernels for 0% -> 0%
where the time goes in v3:
time: 211 us; the launch traced here: 210 us
  Pallas kernels  193 us (91%)
  other arithmetic  15.4 us (7%)
  local copies, waits for them, and re-layouts  2.33 us (1%)
    pallas_call x1, Pallas kernels, play_rounds(): pl.pallas_call(rounds_kernel, out_shape=[jax.ShapeDtypeStruct(top.shape,...  120 us
    pallas_call x1, Pallas kernels, regroup(): pl.pallas_call(regroup_kernel, out_shape=[jax.ShapeDtypeStruct((rows, wid...  73 us
    convert_element_type x1, other arithmetic, standardize(): return (centred / jnp.sqrt(col_var + epsilon)).astype(jnp.bfloat16)  4.58 us

profile of v3, /device:TPU:1, one launch (start us, length us, event | category | flops | bytes accessed | tf_op | source)
XLA Modules:
  0.0 210.4 jit_solution(13050771661173306955)
XLA Ops:
  0.0 0.0 copy-start
  0.0 0.1 broadcast_add_fusion
  0.1 4.1 %convert_reduce_fusion = f32[512]{0:T(512)S(1)} fusion(s32[4096,512]{1,0:T(8,128)} %param.2), kind=kLoop, calls=%fused_computation.3 | loop fusion | flops 4193792 | bytes 8390656 | tf_op jit(solution)/shard_map/reduce_sum | solution.py:17
  4.3 0.0 copy-start.1
  4.3 1.5 copy-done
  5.8 1.2 multiply_reduce_fusion
  6.9 0.0 copy-done.1
  6.9 0.1 reshape.121
  7.1 0.1 copy.12
  7.2 0.1 add_select_fusion
  7.3 0.1 copy.9
  7.4 0.1 rev.3
  7.5 0.1 fusion.1
  7.7 0.1 copy.10
  7.8 0.8 fusion.2
  8.5 1.4 pad_add_fusion.choice
  10.0 4.6 %divide_convert_fusion = bf16[4096,512]{1,0:T(8,128)(2,1)S(1)} fusion(s32[4096,512]{1,0:T(8,128)} %param.2, f32[512]{0:T(512)S(1)} %add_sqrt_fusion, f32[512]{0:T(512)S(1)} %broadcast_multiply_fusion), kind=kLoop, calls=%fused_computation | loop fusion | flops 8388608 | bytes 12587008 | tf_op jit(solution)/shard_map/convert_element_type | solution.py:20
  14.6 0.3 fusion.8
  14.9 0.7 broadcast_select_fusion.slots
  15.5 73.0 %shard_map.28 = (bf16[4096,256]{1,0:T(8,128)(2,1)S(1)}, bf16[4096,256]{1,0:T(8,128)(2,1)S(1)}) custom-call(s32[4]{0:T(128)S(1)} %pad_add_fusion.choice, bf16[3,4096,256]{2,1,0:T(8,128)(2,1)S(1)} %broadcast_select_fusion.slots), custom_call_target="tpu_custom_call" | custom-call | tf_op jit(solution)/shard_map/pallas_call | solution.py:380
  88.6 119.5 %shard_map.29 = (bf16[4096,256]{1,0:T(8,128)(2,1)S(1)}, bf16[4096,256]{1,0:T(8,128)(2,1)S(1)}) custom-call(bf16[4096,256]{1,0:T(8,128)(2,1)S(1)} %get-tuple-element.9.top_in, bf16[4096,256]{1,0:T(8,128)(2,1)S(1)} %get-tuple-element.10.low_in), custom_call_target="tpu_custom_call" | custom-call | tf_op jit(solution)/shard_map/pallas_call | solution.py:243
  208.1 2.3 %pad_maximum_fusion = bf16[4096,512]{1,0:T(8,128)(2,1)} fusion(bf16[4096,256]{1,0:T(8,128)(2,1)S(1)} %get-tuple-element.12, bf16[4096,256]{1,0:T(8,128)(2,1)S(1)} %get-tuple-element.11), kind=kLoop, calls=%fused_computation.5 | loop fusion | flops 8388608 | bytes 8388608 | tf_op jit(solution)/shard_map/concatenate | solution.py:440
  (10 shorter events, 0.1 us)
Async XLA Ops:
  0.0 5.8 %copy-start = (s32[4096,512]{1,0:T(8,128)S(1)}, s32[4096,512]{1,0:T(8,128)}, u32[]{:S(2)}) copy-start(s32[4096,512]{1,0:T(8,128)} %param.2) | copy-start | bytes 25165828
  4.3 2.7 %copy-start.1 = (s32[256]{0:T(256)S(1)}, s32[256]{0:T(256)}, u32[]{:S(2)}) copy-start(s32[256]{0:T(256)} %param.3) | copy-start | bytes 3076

commit v4 on v2

v4 whole, which is shorter than its diff:
```python
import jax
import jax.numpy as jnp
from jax import lax
from jax.experimental import pallas as pl
from jax.experimental.pallas import tpu as pltpu
from jax.sharding import PartitionSpec as P

ROUNDS = 3
HALF = 64
CHUNK = 512
AHEAD = 4

epsilon = 1e-05


def product(left, right, left_dim, right_dim):
    dims = (((left_dim,), (right_dim,)), ((), ()))
    return lax.dot_general(
        left, right, dims, precision=lax.Precision.HIGHEST, preferred_element_type=jnp.float32
    )


def spread(tile, row):
    return jnp.broadcast_to(tile[row : row + 1, :], tile.shape)


def inverse_factor_pair(rows):
    lane = lax.broadcasted_iota(jnp.int32, (8, 128), 1)
    sub = lax.broadcasted_iota(jnp.int32, (8, 128), 0)
    start = jnp.where(lane < HALF, 0, HALF)
    col = lane - start
    rows = list(rows)
    pivots = [jnp.ones((8, 128), jnp.float32)] * 8
    for first in range(0, HALF, 8):
        tile = first // 8
        cols = [
            [jnp.take_along_axis(rows[r], start + (first + m), axis=1) for r in range(tile, 8)]
            for m in range(8)
        ]
        for m in range(8):
            here = col == first + m
            pivot = spread(cols[m][0], m)
            inverse = 1.0 / pivot
            pivots[tile] = jnp.where(sub == m, pivot, pivots[tile])
            cols[m][0] = jnp.where(sub > m, cols[m][0], 0.0)
            for n in range(m + 1, 8):
                ratio = spread(cols[n][0], m) * inverse
                cols[n] = [c - f * ratio for c, f in zip(cols[n], cols[m])]
            scaled = jnp.where(here, 1.0, spread(rows[tile], m)) * inverse
            for r in range(tile, 8):
                rows[r] = jnp.where(here, 0.0, rows[r]) - cols[m][r - tile] * scaled
    done = []
    for r in range(8):
        row = sub + 8 * r
        scale = lax.rsqrt(pivots[r])
        done.append(jnp.where(col < row, rows[r] * scale, jnp.where(col == row, scale, 0.0)))
    return jnp.concatenate(done, axis=0)


def diagonal_pair(packed):
    lane = lax.broadcasted_iota(jnp.int32, packed.shape, 1)
    first = lax.rem(lane, 2 * HALF) < HALF
    return jnp.concatenate([jnp.where(first, packed, 0.0), jnp.where(first, 0.0, packed)], axis=0)


def invert_factors(matrices):
    width = matrices[0].shape[0]
    count = width // HALF
    parts = range(0, width, HALF)
    grid = [
        [jnp.concatenate([m[i : i + HALF, j : j + HALF] for m in matrices], axis=1) for j in parts] for i in parts
    ]
    lane = lax.broadcasted_iota(jnp.int32, (HALF, 2 * HALF), 1)
    eye = (lax.broadcasted_iota(jnp.int32, lane.shape, 0) == lax.rem(lane, HALF)).astype(jnp.float32)
    none = jnp.zeros(lane.shape, jnp.float32)
    done = []
    for k in range(count):
        both = inverse_factor_pair([grid[k][k][8 * r : 8 * r + 8] for r in range(8)])
        row = jnp.concatenate([eye if j == k else grid[k][j] for j in range(count)], axis=1)
        panel = product(both, diagonal_pair(row), 1, 0)
        if k + 1 < count:
            corner, spread_panel = diagonal_pair(both), diagonal_pair(panel)
            for i in range(k + 1, count):
                below = product(product(grid[i][k], corner, 1, 1), spread_panel, 1, 0)
                grid[i][k] = none
                grid[i] = [grid[i][j] - below[:, 2 * HALF * j : 2 * HALF * (j + 1)] for j in range(count)]
        done.append([panel[:, 2 * HALF * j : 2 * HALF * (j + 1)] if j <= k else none for j in range(count)])
    return [
        jnp.concatenate(
            [jnp.concatenate([b[:, HALF * m : HALF * (m + 1)] for b in blocks], axis=1) for blocks in done], axis=0
        )
        for m in range(2)
    ]


def rotation_into(turns, r, cross, norm, right_is_there):
    width = cross.shape[0]
    norm_top = jnp.broadcast_to(jnp.sum(norm[0], axis=0, keepdims=True), (width, width)).T
    norm_low = jnp.sum(norm[1], axis=0, keepdims=True)
    coupling = 2.0 * cross[...] / (norm_top + norm_low + epsilon)
    cross[...] = coupling
    row = lax.broadcasted_iota(jnp.int32, (width, width), 0)
    eye = (row == lax.broadcasted_iota(jnp.int32, (width, width), 1)).astype(jnp.float32)
    top_inverse, low_inverse = invert_factors(
        [eye + product(coupling, coupling, 1, 1), eye + product(coupling, coupling, 0, 0)]
    )
    turns[r, 1, 0:width, :] = product(cross[...], low_inverse, 1, 1).astype(jnp.bfloat16)
    turns[r, 1, width:, :] = low_inverse.T.astype(jnp.bfloat16)
    right_is_there()
    turns[r, 0, 0:width, :] = top_inverse.T.astype(jnp.bfloat16)
    turns[r, 0, width:, :] = (-product(cross[...], top_inverse, 0, 1)).astype(jnp.bfloat16)


def own_ring_position():
    group, pair = lax.axis_index("group"), lax.axis_index("pair")
    return (group // 2) * 2 + lax.rem(pair, 2), lax.rem(group, 2)


def whole_kernel(
    choice, counts, top_out, low_out,
    read, slots, landed, passed, tops, lows, staged, shadow, shadow_low, cross, norm, turns, shadow_turns,
    read_sem, send, recv, pass_send, copy_send, copy_recv, move_send, move_recv, after_send, after_recv,
    turn_send, turn_recv, top_send, top_recv, low_send, low_recv,
):
    rows, width = tops.shape[1:]
    chunks = rows // CHUNK
    y, core = own_ring_position()
    side = lax.rem(y, 2)
    column = lax.axis_index("pair") // 2
    even = core == 0

    def device(ahead, y, core):
        y = lax.rem(y + 4, 4)
        there = lax.rem(column + ahead + 16, 16)
        return {"group": (y // 2) * 2 + core, "pair": there * 2 + lax.rem(y, 2)}

    def part(i):
        return pl.ds(pl.multiple_of(i * CHUNK, CHUNK), CHUNK)

    def reading(i):
        return pltpu.make_async_copy(counts.at[part(i)], read.at[part(i)], read_sem.at[i])

    @pl.loop(0, chunks)
    def _(i):
        reading(i).start()

    partner = device(0, y, 1 - core)
    after = device(1, y, 0)
    base = y - side
    top_device = device(0, base + core, side)
    low_device = device(core, base + 1 - core, side)
    low_source = device(side - 1, base + core, 1 - side)

    barrier = pltpu.get_barrier_semaphore()
    others = [partner, low_device, low_source]
    others += [device(0, y + step, c) for step in (1, -1) for c in (0, 1)]
    others += [device(step, y, c) for step in (1, -1) for c in (0, 1)]
    for other in others:
        pl.semaphore_signal(barrier, inc=1, device_id=other)

    @pl.when(core != side)
    def _():
        pl.semaphore_signal(barrier, inc=1, device_id=top_device)
        pl.semaphore_wait(barrier, len(others) + 1)

    @pl.when(core == side)
    def _():
        pl.semaphore_wait(barrier, len(others))


    def away(slot, i):
        place = core if slot == 1 else 2 + core
        return pltpu.make_async_remote_copy(
            src_ref=slots.at[slot, part(i)],
            dst_ref=landed.at[place, part(i)],
            send_sem=send.at[slot, i],
            recv_sem=recv.at[place, i],
            device_id=device(0, y + (1 if slot == 1 else -1), side),
        )

    def across(i):
        return pltpu.make_async_remote_copy(
            src_ref=slots.at[0, part(i)],
            dst_ref=landed.at[core, part(i)],
            send_sem=send.at[0, i],
            recv_sem=recv.at[core, i],
            device_id=partner,
        )

    def stay(i):
        return pltpu.make_async_copy(slots.at[0, part(i)], landed.at[core, part(i)], recv.at[core, i])

    def onward(way, i):
        return pltpu.make_async_remote_copy(
            src_ref=passed.at[way, part(i)],
            dst_ref=landed.at[2 + way, part(i)],
            send_sem=pass_send.at[way, i],
            recv_sem=recv.at[2 + way, i],
            device_id=device(0, y + (1 if way == 0 else -1), core),
        )

    def arrival(place, i):
        here = landed.at[place, part(i)]
        pltpu.make_async_copy(here, here, recv.at[place, i]).wait()


    def copied(m, i):
        source = tops if m == 0 else lows
        return pltpu.make_async_remote_copy(
            src_ref=source.at[0, part(i)],
            dst_ref=shadow.at[m, part(i)],
            send_sem=copy_send.at[m, i],
            recv_sem=copy_recv.at[m, i],
            device_id=after,
        )

    def turned(k):
        r, half = ((0, 1), (0, 0), (1, 1))[k]
        return pltpu.make_async_remote_copy(
            src_ref=turns.at[r, half],
            dst_ref=shadow_turns.at[k],
            send_sem=turn_send.at[k],
            recv_sem=turn_recv.at[k],
            device_id=after,
        )

    def followed(i):
        return pltpu.make_async_remote_copy(
            src_ref=staged.at[0, part(i)],
            dst_ref=shadow_low.at[part(i)],
            send_sem=after_send.at[i],
            recv_sem=after_recv.at[i],
            device_id=after,
        )

    def move(r, i):
        return pltpu.make_async_remote_copy(
            src_ref=staged.at[r, part(i)],
            dst_ref=lows.at[r + 1, part(i)],
            send_sem=move_send.at[r, i],
            recv_sem=move_recv.at[r, i],
            device_id=partner,
        )

    def top_home(i):
        return pltpu.make_async_remote_copy(
            src_ref=tops.at[1, part(i)],
            dst_ref=top_out.at[part(i)],
            send_sem=top_send.at[i],
            recv_sem=top_recv.at[i],
            device_id=top_device,
        )

    def top_stays(i):
        return pltpu.make_async_copy(tops.at[1, part(i)], top_out.at[part(i)], top_recv.at[i])

    def low_home(i):
        return pltpu.make_async_remote_copy(
            src_ref=staged.at[ROUNDS - 1, part(i)],
            dst_ref=low_out.at[part(i)],
            send_sem=low_send.at[i],
            recv_sem=low_recv.at[i],
            device_id=low_device,
        )


    def gather_sums(i, sums):
        reading(i).wait()
        values = read[part(i), :].astype(jnp.float32).reshape(CHUNK // 8, 8, 2 * width)
        return sums[0] + jnp.sum(values, axis=0), sums[1] + jnp.sum(values * values, axis=0)

    nothing = jnp.zeros((8, 2 * width), jnp.float32)
    sums = lax.fori_loop(0, chunks, gather_sums, (nothing, nothing))
    total, squares = (jnp.sum(one, axis=0, keepdims=True) for one in sums)
    mean = total * (1.0 / rows)
    whole = total.astype(jnp.int32)
    spread_of = (rows * squares.astype(jnp.int32) - whole * whole).astype(jnp.float32)
    factor = 1.0 / jnp.sqrt(spread_of * (1.0 / (rows * rows)) + epsilon)

    @pl.loop(0, chunks)
    def _(i):
        scaled = ((read[part(i), :].astype(jnp.float32) - mean) * factor).astype(jnp.bfloat16)
        for slot in range(3):
            slots[slot, part(i), :] = jnp.where(choice[4 + slot] > 0, scaled[:, :width], scaled[:, width:])

        @pl.when(i < AHEAD)
        def _():
            away(1, i).start()
            away(2, i).start()

        @pl.when(core == side)
        def _():
            stay(i).start()

        @pl.when(core != side)
        def _():
            across(i).start()

    def add_products(blocks):
        cross[...] += lax.dot_general(
            *blocks, (((0,), (0,)), ((), ())), preferred_element_type=jnp.float32
        )
        for m, block in enumerate(blocks):
            wide = block.astype(jnp.float32)
            norm[m] += jnp.sum((wide * wide).reshape(CHUNK // 8, 8, width), axis=0)

    def clear_products():
        cross[...] = jnp.zeros_like(cross)
        norm[...] = jnp.zeros_like(norm)

    clear_products()

    @pl.loop(0, chunks)
    def _(i):
        for way in range(2):
            for place in (2 * way, 2 * way + 1):
                arrival(place, i)

            @pl.when(core != side)
            def _():
                first, second = landed[2 * way, part(i)], landed[2 * way + 1, part(i)]
                passed[way, part(i)] = jnp.where(choice[way] > 0, second, first)
                onward(way, i).start()

        @pl.when(i < chunks - AHEAD)
        def _():
            away(1, i + AHEAD).start()
            away(2, i + AHEAD).start()

        blocks = []
        for place, target in ((2, tops), (3, lows)):
            which = choice[place]
            lower = jnp.where(which == 0, landed[0, part(i)], landed[1, part(i)])
            upper = jnp.where(which == 2, landed[2, part(i)], landed[3, part(i)])
            block = jnp.where(which < 2, lower, upper)
            target[0, part(i), :] = block
            blocks.append(block)

        @pl.when(jnp.logical_not(even))
        def _():
            copied(0, i).start()
            copied(1, i).start()

        add_products(blocks)

    def matmul(left, right, turn):
        joined = jnp.concatenate([left, right], axis=1)
        return jnp.dot(joined, turn, preferred_element_type=jnp.float32).astype(jnp.bfloat16)

    @pl.loop(0, ROUNDS)
    def _(r):
        here = jnp.minimum(r, 1)

        @pl.when(r > 0)
        def _():
            clear_products()

            @pl.when(even & (r == 1))
            def _():
                turned(0).wait_recv()

            @pl.when(even & (r == 2))
            def _():
                turned(1).wait_recv()

                @pl.loop(0, chunks)
                def _(i):
                    shadow[0, part(i)] = matmul(shadow[0, part(i)], shadow[1, part(i)], shadow_turns[1])

                turned(2).wait_recv()

            @pl.loop(0, chunks)
            def _(i):
                @pl.when(jnp.logical_not(even))
                def _():
                    move(r - 1, i).wait_recv()

                @pl.when(even & (r == 1))
                def _():
                    copied(0, i).wait_recv()
                    copied(1, i).wait_recv()
                    lows[1, part(i), :] = matmul(shadow[0, part(i)], shadow[1, part(i)], shadow_turns[0])

                @pl.when(even & (r == 2))
                def _():
                    followed(i).wait_recv()
                    lows[2, part(i), :] = matmul(shadow[0, part(i)], shadow_low[part(i)], shadow_turns[2])

                add_products([tops[1, part(i), :], lows[r, part(i), :]])

        def send_right():
            @pl.when(jnp.logical_not(even) & (r == 0))
            def _():
                turned(0).start()

            @pl.when(jnp.logical_not(even) & (r == 1))
            def _():
                turned(2).start()

        rotation_into(turns, r, cross, norm, send_right)

        @pl.when(jnp.logical_not(even) & (r == 0))
        def _():
            turned(1).start()

        @pl.loop(0, chunks)
        def _(i):
            top, low = tops[here, part(i), :], lows[r, part(i), :]

            @pl.when(even | (r == ROUNDS - 1))
            def _():
                staged[r, part(i), :] = matmul(top, low, turns[r, 1])

            @pl.when(even & (r < ROUNDS - 1))
            def _():
                move(r, i).start()

            @pl.when(even & (r == 0))
            def _():
                followed(i).start()

            @pl.when(r == ROUNDS - 1)
            def _():
                low_home(i).start()

            tops[1, part(i), :] = matmul(top, low, turns[r, 0])

            @pl.when((r == ROUNDS - 1) & (core != side))
            def _():
                top_home(i).start()

            @pl.when((r == ROUNDS - 1) & (core == side))
            def _():
                top_stays(i).start()

    @pl.when(jnp.logical_not(even))
    def _():
        for k in range(3):
            turned(k).wait_send()

    @pl.loop(0, chunks)
    def _(i):
        for slot in (1, 2):
            away(slot, i).wait_send()

        @pl.when(core != side)
        def _():
            across(i).wait_send()
            for way in range(2):
                onward(way, i).wait_send()
            top_home(i).wait()

        @pl.when(core == side)
        def _():
            top_stays(i).wait()

        @pl.when(even)
        def _():
            followed(i).wait_send()
            for r in range(ROUNDS - 1):
                move(r, i).wait_send()

        @pl.when(jnp.logical_not(even))
        def _():
            copied(0, i).wait_send()
            copied(1, i).wait_send()

        low_home(i).wait()


def play(choice, counts):
    rows, width = counts.shape[0], counts.shape[1] // 2
    chunks = rows // CHUNK
    anywhere = pl.BlockSpec(memory_space=pl.ANY)

    def blocks(count):
        return pltpu.VMEM((count, rows, width), jnp.bfloat16)

    def dma(*shape):
        return pltpu.SemaphoreType.DMA(shape)

    return pl.pallas_call(
        whole_kernel,
        out_shape=[jax.ShapeDtypeStruct((rows, width), jnp.bfloat16)] * 2,
        in_specs=[pl.BlockSpec(memory_space=pltpu.SMEM), anywhere],
        out_specs=[anywhere, anywhere],
        scratch_shapes=[
            pltpu.VMEM((rows, 2 * width), jnp.int32),
            blocks(3),
            blocks(4),
            blocks(2),
            blocks(2),
            blocks(ROUNDS),
            blocks(ROUNDS),
            blocks(2),
            pltpu.VMEM((rows, width), jnp.bfloat16),
            pltpu.VMEM((width, width), jnp.float32),
            pltpu.VMEM((2, 8, width), jnp.float32),
            pltpu.VMEM((ROUNDS, 2, 2 * width, width), jnp.bfloat16),
            pltpu.VMEM((3, 2 * width, width), jnp.bfloat16),
            dma(chunks),
            dma(3, chunks),
            dma(4, chunks),
            dma(2, chunks),
            dma(2, chunks),
            dma(2, chunks),
            dma(ROUNDS - 1, chunks),
            dma(ROUNDS - 1, chunks),
            dma(chunks),
            dma(chunks),
            dma(3),
            dma(3),
            dma(chunks),
            dma(chunks),
            dma(chunks),
            dma(chunks),
        ],
        compiler_params=pltpu.CompilerParams(
            collective_id=0, has_side_effects=True, vmem_limit_bytes=60 * 2**20
        ),
    )(choice, counts)


def slot_codes(dest_group):
    table = dest_group.reshape(4, 32, 2)
    chip = (jnp.arange(4)[:, None] // 2) * 2 + jnp.arange(32)[None, :] % 2
    distance = (table - chip[:, :, None] + 4) % 4
    other = distance[:, :, ::-1]
    slot = jnp.where(distance == 3, 2, distance)
    slot = jnp.where(distance == 2, jnp.where(other == 1, 2, 1), slot)
    return table, distance, slot


def choices(table, distance, slot):
    y, core = own_ring_position()
    column = lax.axis_index("pair") // 2
    pair = column * 2 + core
    dist, slots, dest = (
        lax.dynamic_index_in_dim(array, pair, 1, keepdims=False) for array in (distance, slot, table)
    )
    far = jnp.where(dist == 2, slots, 0)
    after, before = ((y + 3) % 4) // 2 * 2 + 1, ((y + 1) % 4) // 2 * 2 + 1
    second = jnp.arange(4)
    pass_up = jnp.sum(jnp.where((second == after)[:, None] & (far == 1), 1, 0))
    pass_down = jnp.sum(jnp.where((second == before)[:, None] & (far == 2), 1, 0))
    origin = second % 2
    place = jnp.where(
        dist % 2 == 1,
        origin[:, None] + jnp.where(dist == 1, 0, 2),
        jnp.where(dist == 0, origin[:, None], 1 + slots),
    )
    wanted = jnp.sum(jnp.where(dest == y, place, 0), axis=0)
    return jnp.stack([pass_up, pass_down, wanted[0], wanted[1]]).astype(jnp.int32)


def body(genotypes, dest_group):
    table, distance, slot = slot_codes(dest_group)
    own_slot = lax.dynamic_index_in_dim(slot, lax.axis_index("pair"), 1, keepdims=False)
    own_slot = lax.dynamic_index_in_dim(own_slot, lax.axis_index("group"), 0, keepdims=False)
    takes_first = (jnp.arange(3) == own_slot[0]).astype(jnp.int32)
    choice = jnp.concatenate([choices(table, distance, slot), takes_first])
    top, low = play(choice, genotypes)
    return jnp.concatenate([top, low], axis=1)


def solution(mesh):
    in_specs = (P(None, ("group", "pair")), P())
    out_specs = P(None, ("group", "pair"))
    return jax.shard_map(body, mesh=mesh, in_specs=in_specs, out_specs=out_specs, check_vma=False)
```

time: 253 us -> 204 us (0.81)
  waiting for transfers between devices: 93.9 us -> 0 us
  Pallas kernels: 122 us -> 195 us
  starting transfers between devices: 17.5 us -> 0 us
  other arithmetic: 15.4 us -> 7.58 us
    ppermute x4 -> x0, waiting for transfers between devices: 93.9 us -> none  [moved(): return lax.ppermute(array, ('group', 'pair'), pairs)]
    pallas_call x4 -> x1, Pallas kernels: 122 us -> 195 us  [play(): pl.pallas_call(whole_kernel, out_shape=[jax.ShapeDtypeStruct((rows, width...]
    ppermute x4 -> x0, starting transfers between devices: 17.5 us -> none  [moved(): return lax.ppermute(array, ('group', 'pair'), pairs)]
    reduce_sum x2 -> x0, other arithmetic: 5.3 us -> none  [the longest x1 4.15 us: standardize(): col_mean = jnp.mean(values, axis=0)]
    convert_element_type x1, other arithmetic: 4.58 us -> 0.04 us  [body(): takes_first = (jnp.arange(3) == own_slot[0]).astype(jnp.int32)]
  transfers between devices with their start and end apart: 4 -> 0, of which waited for: 4 -> 0; matrix products, arithmetic and copies ran while one was open for 0% -> 0% of each run, Pallas kernels for 0% -> 0%
where the time goes in v4:
time: 204 us; the launch traced here: 203 us
  Pallas kernels  195 us (96%)
  other arithmetic  7.58 us (4%)
    pallas_call x1, Pallas kernels, play(): pl.pallas_call(whole_kernel, out_shape=[jax.ShapeDtypeStruct((rows, width...  195 us
    concatenate x1, other arithmetic, body(): return jnp.concatenate([top, low], axis=1)  4.54 us

profile of v4, /device:TPU:1, one launch (start us, length us, event | category | flops | bytes accessed | tf_op | source)
XLA Modules:
  0.0 203.4 jit_solution(7231922231271486234)
XLA Ops:
  0.0 0.1 broadcast_add_fusion
  0.1 0.8 reshape.107
  0.9 0.1 copy.12
  1.0 0.1 add_select_fusion
  1.2 0.1 copy.9
  1.3 0.1 rev.3
  1.3 0.1 fusion.1
  1.5 0.1 copy.10
  1.6 0.8 fusion.2
  2.4 1.9 pad_add_fusion.choice
  4.3 194.5 %shard_map.28 = (bf16[4096,256]{1,0:T(8,128)(2,1)}, bf16[4096,256]{1,0:T(8,128)(2,1)}) custom-call(s32[7]{0:T(128)} %pad_add_fusion.choice, s32[4096,512]{1,0:T(8,128)} %counts.1), custom_call_target="tpu_custom_call" | custom-call | tf_op jit(solution)/shard_map/pallas_call | solution.py:482
  198.9 4.5 %pad_maximum_fusion = bf16[4096,512]{1,0:T(8,128)(2,1)} fusion(bf16[4096,256]{1,0:T(8,128)(2,1)} %get-tuple-element.8, bf16[4096,256]{1,0:T(8,128)(2,1)} %get-tuple-element.7), kind=kLoop, calls=%fused_computation | loop fusion | flops 8388608 | bytes 8388608 | tf_op jit(solution)/shard_map/concatenate | solution.py:563
  (8 shorter events, 0.1 us)

commit v5 on v4

--- a/solution.py
+++ b/solution.py
@@ -8,7 +8,7 @@
 ROUNDS = 3
 HALF = 64
 CHUNK = 512
-AHEAD = 4
+AHEAD = 2
 
 epsilon = 1e-05
 
@@ -117,7 +117,7 @@
 
 
 def whole_kernel(
-    choice, counts, top_out, low_out,
+    dest, counts, top_out, low_out,
     read, slots, landed, passed, tops, lows, staged, shadow, shadow_low, cross, norm, turns, shadow_turns,
     read_sem, send, recv, pass_send, copy_send, copy_recv, move_send, move_recv, after_send, after_recv,
     turn_send, turn_recv, top_send, top_recv, low_send, low_recv,
@@ -128,6 +128,7 @@
     side = lax.rem(y, 2)
     column = lax.axis_index("pair") // 2
     even = core == 0
+    pass_second, wanted, first_slot = choices(dest)
 
     def device(ahead, y, core):
         y = lax.rem(y + 4, 4)
@@ -281,7 +282,7 @@
     def _(i):
         scaled = ((read[part(i), :].astype(jnp.float32) - mean) * factor).astype(jnp.bfloat16)
         for slot in range(3):
-            slots[slot, part(i), :] = jnp.where(choice[4 + slot] > 0, scaled[:, :width], scaled[:, width:])
+            slots[slot, part(i), :] = jnp.where(first_slot == slot, scaled[:, :width], scaled[:, width:])
 
         @pl.when(i < AHEAD)
         def _():
@@ -319,7 +320,7 @@
             @pl.when(core != side)
             def _():
                 first, second = landed[2 * way, part(i)], landed[2 * way + 1, part(i)]
-                passed[way, part(i)] = jnp.where(choice[way] > 0, second, first)
+                passed[way, part(i)] = jnp.where(pass_second[way] > 0, second, first)
                 onward(way, i).start()
 
         @pl.when(i < chunks - AHEAD)
@@ -328,8 +329,7 @@
             away(2, i + AHEAD).start()
 
         blocks = []
-        for place, target in ((2, tops), (3, lows)):
-            which = choice[place]
+        for which, target in zip(wanted, (tops, lows)):
             lower = jnp.where(which == 0, landed[0, part(i)], landed[1, part(i)])
             upper = jnp.where(which == 2, landed[2, part(i)], landed[3, part(i)])
             block = jnp.where(which < 2, lower, upper)
@@ -468,7 +468,7 @@
         low_home(i).wait()
 
 
-def play(choice, counts):
+def play(dest, counts):
     rows, width = counts.shape[0], counts.shape[1] // 2
     chunks = rows // CHUNK
     anywhere = pl.BlockSpec(memory_space=pl.ANY)
@@ -516,50 +516,49 @@
             dma(chunks),
         ],
         compiler_params=pltpu.CompilerParams(
-            collective_id=0, has_side_effects=True, vmem_limit_bytes=60 * 2**20
+            collective_id=0, has_side_effects=True, vmem_limit_bytes=55 * 2**20
         ),
-    )(choice, counts)
-
-
-def slot_codes(dest_group):
-    table = dest_group.reshape(4, 32, 2)
-    chip = (jnp.arange(4)[:, None] // 2) * 2 + jnp.arange(32)[None, :] % 2
-    distance = (table - chip[:, :, None] + 4) % 4
-    other = distance[:, :, ::-1]
-    slot = jnp.where(distance == 3, 2, distance)
-    slot = jnp.where(distance == 2, jnp.where(other == 1, 2, 1), slot)
-    return table, distance, slot
-
-
-def choices(table, distance, slot):
+    )(dest, counts)
+
+
+def routed(dest, group, pair, side):
+    chip = (group // 2) * 2 + lax.rem(pair, 2)
+    distance, other = (lax.rem(dest[(group * 32 + pair) * 2 + k] - chip + 4, 4) for k in (side, 1 - side))
+    slot = jnp.where(distance == 2, jnp.where(other == 1, 2, 1), jnp.where(distance == 3, 2, distance))
+    return distance, slot
+
+
+def choices(dest):
     y, core = own_ring_position()
-    column = lax.axis_index("pair") // 2
-    pair = column * 2 + core
-    dist, slots, dest = (
-        lax.dynamic_index_in_dim(array, pair, 1, keepdims=False) for array in (distance, slot, table)
+    group, own_pair = lax.axis_index("group"), lax.axis_index("pair")
+    pair = (own_pair // 2) * 2 + core
+
+    def passing(chip, slot):
+        distance, used = routed(dest, (chip // 2) * 2 + 1, pair, 0)
+        other, other_used = routed(dest, (chip // 2) * 2 + 1, pair, 1)
+        far = ((distance == 2) & (used == slot)) | ((other == 2) & (other_used == slot))
+        return far.astype(jnp.int32)
+
+    def landing(side):
+        found = jnp.int32(0)
+        for source in range(4):
+            distance, slot = routed(dest, source, pair, side)
+            origin = source % 2
+            near = jnp.where(distance == 1, origin, 2 + origin)
+            place = jnp.where(lax.rem(distance, 2) == 1, near, jnp.where(distance == 0, origin, 1 + slot))
+            found = found + jnp.where(dest[(source * 32 + pair) * 2 + side] == y, place, 0)
+        return found
+
+    first = routed(dest, group, own_pair, 0)[1]
+    return (
+        (passing(lax.rem(y + 3, 4), 1), passing(lax.rem(y + 1, 4), 2)),
+        (landing(0), landing(1)),
+        first,
     )
-    far = jnp.where(dist == 2, slots, 0)
-    after, before = ((y + 3) % 4) // 2 * 2 + 1, ((y + 1) % 4) // 2 * 2 + 1
-    second = jnp.arange(4)
-    pass_up = jnp.sum(jnp.where((second == after)[:, None] & (far == 1), 1, 0))
-    pass_down = jnp.sum(jnp.where((second == before)[:, None] & (far == 2), 1, 0))
-    origin = second % 2
-    place = jnp.where(
-        dist % 2 == 1,
-        origin[:, None] + jnp.where(dist == 1, 0, 2),
-        jnp.where(dist == 0, origin[:, None], 1 + slots),
-    )
-    wanted = jnp.sum(jnp.where(dest == y, place, 0), axis=0)
-    return jnp.stack([pass_up, pass_down, wanted[0], wanted[1]]).astype(jnp.int32)
 
 
 def body(genotypes, dest_group):
-    table, distance, slot = slot_codes(dest_group)
-    own_slot = lax.dynamic_index_in_dim(slot, lax.axis_index("pair"), 1, keepdims=False)
-    own_slot = lax.dynamic_index_in_dim(own_slot, lax.axis_index("group"), 0, keepdims=False)
-    takes_first = (jnp.arange(3) == own_slot[0]).astype(jnp.int32)
-    choice = jnp.concatenate([choices(table, distance, slot), takes_first])
-    top, low = play(choice, genotypes)
+    top, low = play(dest_group, genotypes)
     return jnp.concatenate([top, low], axis=1)
 
 

time: 204 us -> 188 us (0.922)
  Pallas kernels: 195 us -> 184 us
  other arithmetic: 7.58 us -> 4.54 us
    pallas_call x1, Pallas kernels: 195 us -> 184 us  [play(): pl.pallas_call(whole_kernel, out_shape=[jax.ShapeDtypeStruct((rows, width...]
where the time goes in v5:
time: 188 us
  Pallas kernels  184 us (98%)
  other arithmetic  4.54 us (2%)
    pallas_call x1, Pallas kernels, play(): pl.pallas_call(whole_kernel, out_shape=[jax.ShapeDtypeStruct((rows, width...  184 us
    concatenate x1, other arithmetic, body(): return jnp.concatenate([top, low], axis=1)  4.54 us

profile of v5, /device:TPU:1, one launch (start us, length us, event | category | flops | bytes accessed | tf_op | source)
XLA Modules:
  0.0 188.2 jit_solution(17454132723499709238)
XLA Ops:
  0.0 183.6 %shard_map.28 = (bf16[4096,256]{1,0:T(8,128)(2,1)}, bf16[4096,256]{1,0:T(8,128)(2,1)}) custom-call(s32[256]{0:T(256)} %dest.1, s32[4096,512]{1,0:T(8,128)} %counts.1), custom_call_target="tpu_custom_call" | custom-call | tf_op jit(solution)/shard_map/pallas_call | solution.py:482
  183.6 4.5 %pad_maximum_fusion = bf16[4096,512]{1,0:T(8,128)(2,1)} fusion(bf16[4096,256]{1,0:T(8,128)(2,1)} %get-tuple-element.8, bf16[4096,256]{1,0:T(8,128)(2,1)} %get-tuple-element.7), kind=kLoop, calls=%fused_computation | loop fusion | flops 8388608 | bytes 8388608 | tf_op jit(solution)/shard_map/concatenate | solution.py:562

commit v6 on v5

--- a/solution.py
+++ b/solution.py
@@ -118,7 +118,7 @@
 
 def whole_kernel(
     dest, counts, top_out, low_out,
-    read, slots, landed, passed, tops, lows, staged, shadow, shadow_low, cross, norm, turns, shadow_turns,
+    read, slots, landed, passed, tops, lows, shadow, shadow_low, cross, norm, turns, shadow_turns,
     read_sem, send, recv, pass_send, copy_send, copy_recv, move_send, move_recv, after_send, after_recv,
     turn_send, turn_recv, top_send, top_recv, low_send, low_recv,
 ):
@@ -227,7 +227,7 @@
 
     def followed(i):
         return pltpu.make_async_remote_copy(
-            src_ref=staged.at[0, part(i)],
+            src_ref=slots.at[0, part(i)],
             dst_ref=shadow_low.at[part(i)],
             send_sem=after_send.at[i],
             recv_sem=after_recv.at[i],
@@ -236,7 +236,7 @@
 
     def move(r, i):
         return pltpu.make_async_remote_copy(
-            src_ref=staged.at[r, part(i)],
+            src_ref=slots.at[r, part(i)],
             dst_ref=lows.at[r + 1, part(i)],
             send_sem=move_send.at[r, i],
             recv_sem=move_recv.at[r, i],
@@ -257,7 +257,7 @@
 
     def low_home(i):
         return pltpu.make_async_remote_copy(
-            src_ref=staged.at[ROUNDS - 1, part(i)],
+            src_ref=slots.at[ROUNDS - 1, part(i)],
             dst_ref=low_out.at[part(i)],
             send_sem=low_send.at[i],
             recv_sem=low_recv.at[i],
@@ -347,6 +347,15 @@
         joined = jnp.concatenate([left, right], axis=1)
         return jnp.dot(joined, turn, preferred_element_type=jnp.float32).astype(jnp.bfloat16)
 
+    @pl.loop(0, chunks)
+    def _(i):
+        for slot in (1, 2):
+            away(slot, i).wait_send()
+
+        @pl.when(core != side)
+        def _():
+            across(i).wait_send()
+
     @pl.loop(0, ROUNDS)
     def _(r):
         here = jnp.minimum(r, 1)
@@ -409,7 +418,7 @@
 
             @pl.when(even | (r == ROUNDS - 1))
             def _():
-                staged[r, part(i), :] = matmul(top, low, turns[r, 1])
+                slots[r, part(i), :] = matmul(top, low, turns[r, 1])
 
             @pl.when(even & (r < ROUNDS - 1))
             def _():
@@ -440,12 +449,8 @@
 
     @pl.loop(0, chunks)
     def _(i):
-        for slot in (1, 2):
-            away(slot, i).wait_send()
-
         @pl.when(core != side)
         def _():
-            across(i).wait_send()
             for way in range(2):
                 onward(way, i).wait_send()
             top_home(i).wait()
@@ -491,7 +496,6 @@
             blocks(2),
             blocks(2),
             blocks(ROUNDS),
-            blocks(ROUNDS),
             blocks(2),
             pltpu.VMEM((rows, width), jnp.bfloat16),
             pltpu.VMEM((width, width), jnp.float32),
@@ -516,7 +520,7 @@
             dma(chunks),
         ],
         compiler_params=pltpu.CompilerParams(
-            collective_id=0, has_side_effects=True, vmem_limit_bytes=55 * 2**20
+            collective_id=0, has_side_effects=True, vmem_limit_bytes=49 * 2**20
         ),
     )(dest, counts)
 

time: 188 us -> 187 us (level)
  other arithmetic: 4.54 us -> 2.35 us
    concatenate x1, other arithmetic: 4.54 us -> 2.35 us  [body(): return jnp.concatenate([top, low], axis=1)]
where the time goes in v6:
time: 187 us
  Pallas kernels  183 us (98%)
  other arithmetic  2.35 us (1%)
    pallas_call x1, Pallas kernels, play(): pl.pallas_call(whole_kernel, out_shape=[jax.ShapeDtypeStruct((rows, width...  183 us

profile of v6, /device:TPU:1, one launch (start us, length us, event | category | flops | bytes accessed | tf_op | source)
XLA Modules:
  0.0 186.5 jit_solution(10760769583994952767)
XLA Ops:
  0.0 0.0 copy-start
  0.0 0.7 copy-done
  0.7 183.5 %shard_map.28 = (bf16[4096,256]{1,0:T(8,128)(2,1)S(1)}, bf16[4096,256]{1,0:T(8,128)(2,1)S(1)}) custom-call(s32[256]{0:T(256)S(1)} %copy-done, s32[4096,512]{1,0:T(8,128)} %counts.1), custom_call_target="tpu_custom_call" | custom-call | tf_op jit(solution)/shard_map/pallas_call | solution.py:487
  184.2 2.3 %pad_maximum_fusion = bf16[4096,512]{1,0:T(8,128)(2,1)} fusion(bf16[4096,256]{1,0:T(8,128)(2,1)S(1)} %get-tuple-element.8, bf16[4096,256]{1,0:T(8,128)(2,1)S(1)} %get-tuple-element.7), kind=kLoop, calls=%fused_computation | loop fusion | flops 8388608 | bytes 8388608 | tf_op jit(solution)/shard_map/concatenate | solution.py:566
Async XLA Ops:
  0.0 0.7 copy-start
